TPU v7x, 32 devices: a whole 2x2x4 slice. The times are simulated.
32 devices in a mesh: groups: 2 (over x), width: 8 (over z, y), guide: 2 (over core).
Axes of the slice: x: 2, y: 2, z: 4, core: 2. Of those that a mesh axis runs over, the one named last changes fastest.
Arguments:
- latent: float32 [16, 8, 2048], P(None, None, ('groups', 'width')), parts along dimension 2, may hold values from -6 to 6
- starts: int32 [16], P(('groups', 'width')), parts along dimension 0, may hold values from 0 to 1023, as said below
- counts: int32 [2048], P(('groups', 'width')), parts along dimension 0, may hold values from 1 to 3, as said below
- step_index: int32 [2], P('groups'), parts along dimension 0, may hold values from 0 to 27
- cond_mod: float32 [2, 3, 2432], P('guide'), may hold values from -3 to 3
- w_patch: bfloat16 [64, 2432], replicated, may hold values from -0.75 to 0.75
- w_qkv: bfloat16 [2432, 3840], P('width'), may hold values from -0.125 to 0.125
- w_out: bfloat16 [1280, 2432], replicated, may hold values from -0.15625 to 0.15625
- w_final: bfloat16 [2432, 64], replicated, may hold values from -0.125 to 0.125
- w_dec: bfloat16 [144, 512], replicated, may hold values from -0.5 to 0.5
Outputs:
- denoised: float32 [16, 8, 2048], P(None, 'guide', ('groups', 'width')), parts along dimension 2
- features: bfloat16 [8, 2048, 512], P('guide', ('groups', 'width')), parts along dimension 1
There are 2 independent parts, one for each index of `groups`. A program takes and returns all parts, laid end to end along the dimension named above; an argument that names none is the same for every part. Nothing has to cross between parts.
Inputs may be any that keep to these rules, and one draw needn't show every extreme that they name: window k starts between column k * 128 and column (k + 1) * 128 - 1 and covers 2 * 128 columns, wrapping around the panorama. `counts`: the number of windows whose columns, as given by starts, include the column.
All inputs are finite; a program needn't handle non-finite values.
Results may differ from a plain program's by a relative error of at most 0.013.
Values may be sent and summed in bfloat16 or wider, within the bound.
A program may use at most 128 MiB of HBM per device.

v0:
```python
import jax
import jax.numpy as jnp
from jax import lax
from jax.sharding import PartitionSpec as P

HEADS = 20
HEAD = 64
STEPS = 28


guidance = 4.0
epsilon = 1e-06


def from_behind(x, axis, by):
    peers = lax.axis_size(axis)
    return lax.ppermute(x, axis, [(i, (i + by) % peers) for i in range(peers)])


def from_partner(block, axis, stride):
    count = lax.axis_size(axis)
    route = []
    for low in range(count):
        high = low | 1 << stride
        if high != low and high < count:
            route += [(low, high), (high, low)]
    return lax.ppermute(block, axis, route)


def extended(block, sides, width):
    for axis, dim in sides:
        count = lax.axis_size(axis)
        forward = [(i, i + 1) for i in range(count - 1)]
        backward = [(target, source) for source, target in forward]
        low = lax.ppermute(
            lax.slice_in_dim(block, block.shape[dim] - width, None, axis=dim), axis, forward
        )
        high = lax.ppermute(lax.slice_in_dim(block, 0, width, axis=dim), axis, backward)
        block = jnp.concatenate([low, block, high], axis=dim)
    return block


def layer_norm(values):
    centered = values - jnp.mean(values, axis=-1, keepdims=True)
    spread = jnp.mean(centered * centered, axis=-1, keepdims=True)
    return centered * lax.rsqrt(spread + epsilon)


def head_norm(values):
    return values * lax.rsqrt(jnp.mean(values * values, axis=-1, keepdims=True) + epsilon)


def patchify(window):
    channels, height, breadth = window.shape
    folded = window.reshape(channels, height // 2, 2, breadth // 2, 2).transpose(1, 3, 2, 4, 0)
    return folded.reshape(height // 2 * (breadth // 2), 4 * channels)


def unpatchify(tokens, channels, height, breadth):
    folded = tokens.reshape(height // 2, breadth // 2, 2, 2, channels).transpose(4, 0, 2, 1, 3)
    return folded.reshape(channels, height, breadth)


def attend(queries, key_rows, value_rows):
    scores = jnp.einsum("bqhe,bkhe->bhqk", queries, key_rows, preferred_element_type=jnp.float32)
    scores = scores / jnp.sqrt(jnp.float32(queries.shape[-1]))
    weights = jax.nn.softmax(scores, axis=-1).astype(jnp.bfloat16)
    mixed = jnp.einsum("bhqk,bkhe->bqhe", weights, value_rows, preferred_element_type=jnp.float32)
    return mixed.astype(jnp.bfloat16)


def convolve(padded, w_dec):
    channels = padded.shape[0]
    height = padded.shape[1] - 2
    breadth = padded.shape[2] - 2
    shifted = [
        padded[:, row_at : row_at + height, col_at : col_at + breadth]
        for row_at in range(3)
        for col_at in range(3)
    ]
    stacked = jnp.stack(shifted).reshape(9 * channels, height * breadth)
    summed = lax.dot_general(
        stacked, w_dec, (((0,), (0,)), ((), ())), preferred_element_type=jnp.float32
    )
    return jax.nn.silu(summed).astype(jnp.bfloat16).reshape(height, breadth, w_dec.shape[1])


def fetch_next(block):
    return from_behind(block, "width", -1)


def pass_right(block):
    return from_behind(block.astype(jnp.bfloat16), "width", 1).astype(block.dtype)


def shards(latent, starts, counts, step_index, cond_mod, w_patch, w_qkv, w_out, w_final, w_dec):
    guide_at = lax.axis_index("guide")
    place = lax.axis_index("width")
    channels, height, columns = latent.shape
    half_rows = height // 2
    fraction = (step_index[0].astype(jnp.float32) + 1.0) / STEPS
    sigma = 3.0 * fraction / (1.0 + 2.0 * fraction)
    modulation = cond_mod[0]
    own_cols = latent.astype(jnp.bfloat16)
    ahead = fetch_next(own_cols)
    further = fetch_next(ahead)
    three_blocks = jnp.concatenate([own_cols, ahead, further], axis=2)
    offset = starts[0] - place * columns
    window = lax.dynamic_slice_in_dim(three_blocks, offset, 2 * columns, 2)
    patches = patchify(window)
    token_count = patches.shape[0]
    hidden = jnp.dot(patches, w_patch, preferred_element_type=jnp.float32)
    modulated = (layer_norm(hidden) * (1.0 + modulation[1]) + modulation[0]).astype(jnp.bfloat16)
    partner = from_partner(modulated, "guide", 0)
    both_rows = jnp.where(
        guide_at == 0, jnp.stack([modulated, partner]), jnp.stack([partner, modulated])
    )
    both_rows = both_rows.reshape(2 * token_count, modulated.shape[1])
    head_share = HEADS // 2
    shard_rows = w_qkv.shape[0]
    weight_half = lax.dynamic_slice_in_dim(
        w_qkv.reshape(shard_rows, 3, HEADS, HEAD), guide_at * head_share, head_share, 2
    )
    weight_half = weight_half.reshape(shard_rows, 3 * head_share * HEAD)
    projected = jnp.dot(
        both_rows,
        lax.all_gather(weight_half, "width", axis=0, tiled=True),
        preferred_element_type=jnp.float32,
    )
    projected = projected.reshape(2, token_count, 3, head_share, HEAD)
    queries = head_norm(projected[:, :, 0]).astype(jnp.bfloat16)
    key_rows = head_norm(projected[:, :, 1]).astype(jnp.bfloat16)
    value_rows = projected[:, :, 2].astype(jnp.bfloat16)
    attended = attend(queries, key_rows, value_rows).reshape(2 * token_count, head_share * HEAD)
    out_rows = lax.dynamic_slice_in_dim(w_out, guide_at * head_share * HEAD, head_share * HEAD, 0)
    partial_value = jnp.dot(attended, out_rows, preferred_element_type=jnp.float32).reshape(
        2, token_count, w_out.shape[1]
    )
    mixed_out = lax.psum_scatter(
        partial_value.astype(jnp.bfloat16), "guide", scatter_dimension=0, tiled=True
    ).astype(jnp.float32)[0]
    residual = hidden + modulation[2] * mixed_out
    final_in = layer_norm(residual).astype(jnp.bfloat16)
    result = jnp.dot(final_in, w_final, preferred_element_type=jnp.float32)
    velocity_win = unpatchify(result, channels, height, 2 * columns)
    branch_pair = lax.all_to_all(
        velocity_win[None].astype(jnp.bfloat16), "guide", split_axis=2, concat_axis=0, tiled=True
    ).astype(jnp.float32)
    guided = branch_pair[1] + guidance * (branch_pair[0] - branch_pair[1])
    spread_out = jnp.zeros((channels, half_rows, 3 * columns), jnp.float32)
    spread_out = lax.dynamic_update_slice_in_dim(spread_out, guided, offset, 2)
    carried = pass_right(spread_out[:, :, 2 * columns :])
    arrived = pass_right(spread_out[:, :, columns : 2 * columns] + carried)
    summed = spread_out[:, :, :columns] + arrived
    velocity = summed / counts.astype(jnp.float32)[None, None, :]
    mine_rows = lax.dynamic_slice_in_dim(latent, guide_at * half_rows, half_rows, 1)
    denoised = mine_rows - sigma * velocity
    padded = extended(denoised.astype(jnp.bfloat16), (("guide", 1), ("width", 2)), 1)
    features = convolve(padded, w_dec)
    return (denoised, features)


def solution(mesh):
    return jax.shard_map(
        shards,
        mesh=mesh,
        in_specs=(
            P(None, None, ("groups", "width")),
            P(("groups", "width")),
            P(("groups", "width")),
            P("groups"),
            P("guide", None, None),
            P(),
            P("width", None),
            P(),
            P(),
            P(),
        ),
        out_specs=(P(None, "guide", ("groups", "width")), P("guide", ("groups", "width"), None)),
        check_vma=False,
    )
```

profile of v0, /device:TPU:0, one launch (start us, length us, event | category | flops | bytes accessed | tf_op | source)
XLA Modules:
  0.0 284.3 jit_solution(5866533222557531510)
XLA Ops:
  7.2 0.0 copy-start
  7.2 0.0 all-gather.2.cloned.1.call-start
  7.3 3.7 %copy.37 = bf16[304,3840]{0,1:T(8,128)(2,1)S(1)} copy(bf16[304,3840]{1,0:T(8,128)(2,1)} %param.16) | data formatting | bytes 4669440 | tf_op args[6]
  10.9 1.3 constant_dynamic-slice_fusion
  12.2 2.5 copy.38
  14.7 0.0 all-gather.2.cloned.1.call-update
  14.8 0.0 reduce-scatter.2.cloned.1.call-start
  14.8 6.1 %collective-permute-start = (bf16[16,8,128]{2,1,0:T(8,128)(2,1)S(1)}, bf16[16,8,128]{2,1,0:T(8,128)(2,1)S(1)}, u32[]{:S(2)}, u32[]{:S(2)}) collective-permute-start(bf16[16,8,128]{2,1,0:T(8,128)(2,1)S(1)} %convert_element_type.86), channel_id=1, source_target_pairs={{0,14},{2,0},{4,2},{6,4},{8,6},{10,8},{12,10},{14,12},{1,15},{3,1}... | collective-permute-start | bytes 98312 | tf_op jit(solution)/shard_map/ppermute | solution.py:17
  20.9 1.6 collective-permute-done
  22.5 5.0 %collective-permute-start.1 = (bf16[16,8,128]{2,1,0:T(8,128)(2,1)S(1)}, bf16[16,8,128]{2,1,0:T(8,128)(2,1)S(1)}, u32[]{:S(2)}, u32[]{:S(2)}) collective-permute-start(bf16[16,8,128]{2,1,0:T(8,128)(2,1)S(1)} %collective-permute-done), channel_id=1, source_target_pairs={{0,14},{2,0},{4,2},{6,4},{8,6},{10,8},{12,10},{14,12},{1,15},{3,1}... | collective-permute-start | bytes 98312 | tf_op jit(solution)/shard_map/ppermute | solution.py:17
  27.5 0.1 slice_reduce_fusion.1
  28.3 1.4 collective-permute-done.1
  29.7 0.1 fusion.33
  29.8 0.3 copy.35
  30.1 0.4 copy.36
  30.5 0.9 fusion.52
  31.4 0.6 multiply_reduce_fusion.2
  32.1 1.0 add_convert_fusion
  33.1 0.6 copy-done.2
  33.6 0.0 collective-permute-start.2
  33.6 4.9 %fusion.59 = bf16[1,512,2432]{2,1,0:T(8,128)(2,1)} fusion(f32[2432]{0:T(1024)S(1)} %get-tuple-element.5, f32[2432]{0:T(1024)S(1)} %get-tuple-element.6, f32[512]{0:T(512)S(1)} %add_rsqrt_fusion.3, f32[512,2432]{1,0:T(8,128)} %copy-done.2, f32[512]{0:T(512)S(1)} %broadcast_multiply_fusion.1), kind=kLoop, calls=%fused_computation.109 | loop fusion | flops 6225920 | bytes 7494656 | tf_op jit(solution)/shard_map/stack | solution.py:116
  38.5 115.2 %all-gather.2.cloned.1.call-done = bf16[2432,1920]{1,0:T(8,128)(2,1)} async-done(((bf16[304,1920]{1,0:T(8,128)(2,1)}), bf16[2432,1920]{1,0:T(8,128)(2,1)}) %all-gather.2.cloned.1.call-update) | async-done | bytes 9338896 | tf_op jit(solution)/shard_map/all_gather | solution.py:127
  153.7 13.3 %copy.39 = bf16[1920,2432]{1,0:T(8,128)(2,1)} copy(bf16[1920,2432]{0,1:T(8,128)(2,1)} %bitcast.153) | data formatting | bytes 18677760 | tf_op jit(solution)/shard_map/dot_general | solution.py:125
  166.9 0.0 collective-permute-done.2
  166.9 23.0 %fusion.7 = f32[2,512,3,10,64]{1,4,3,2,0:T(8,128)S(1)} fusion(bf16[3,10,64,2432,1]{3,2,1,0,4:T(8,128)(2,1)} %bitcast.154, bf16[1,512,2432]{2,1,0:T(8,128)(2,1)} %bitcast.5, bf16[1,512,2432]{2,1,0:T(8,128)(2,1)} %fusion.59, pred[]{:T(512)S(6)} %eq.3), kind=kOutput, calls=%fused_computation.10 | convolution fusion | flops 9585426432 | bytes 22183936 | tf_op jit(solution)/shard_map/dot_general | solution.py:125
  189.9 3.1 %copy-done.4 = f32[2,512,3,10,64]{1,4,3,2,0:T(8,128)} copy-done((f32[2,512,3,10,64]{1,4,3,2,0:T(8,128)}, f32[2,512,3,10,64]{1,4,3,2,0:T(8,128)S(1)}, u32[]{:S(2)}) %copy-start.4) | copy-done | bytes 7864344
  193.1 0.8 multiply_reduce_fusion.3
  193.9 0.0 slice-start.2
  193.9 13.0 %fusion.53 = (f32[2,10,512]{2,1,0:T(8,128)S(1)}, f32[2,10,512,512]{2,3,1,0:T(8,128)}) fusion(f32[2,512,3,10,64]{1,4,3,2,0:T(8,128)} %copy-done.4, f32[2,512,10]{1,2,0:T(8,128)S(1)} %get-tuple-element.20, f32[2,512,10]{1,2,0:T(8,128)S(1)} %get-tuple-element.19), kind=kOutput, calls=%fused_computation.108 | convolution fusion | flops 689439232 | bytes 26337280 | tf_op jit(solution)/shard_map/sub | solution.py:67
  206.8 9.8 %fusion.23 = bf16[2,10,64,512]{3,2,1,0:T(8,128)(2,1)S(1)} fusion(f32[2,10,512,512]{2,3,1,0:T(8,128)} %get-tuple-element.18, f32[2,10,512]{2,1,0:T(8,128)S(1)} %get-tuple-element.17, f32[2,512,3,10,64]{1,4,3,2,0:T(8,128)} %copy-done.4), kind=kOutput, calls=%fused_computation.36 | convolution fusion | flops 682229760 | bytes 23633920 | tf_op jit(solution)/shard_map/bhqk,bkhe->bqhe/dot_general | solution.py:68
  216.7 6.0 %convolution_convert_fusion = bf16[2,512,2432]{2,1,0:T(8,128)(2,1)} fusion(bf16[2,512,640]{1,2,0:T(8,128)(2,1)S(1)} %bitcast.164, bf16[1280,2432]{1,0:T(8,128)(2,1)S(1)} %bitcast.163, s32[]{:T(128)S(6)} %select_n.28), kind=kOutput, calls=%fused_computation.7 | convolution fusion | flops 3190161408 | bytes 9404420 | tf_op jit(solution)/shard_map/dot_general | solution.py:136
  222.7 0.0 reduce-scatter.2.cloned.1.call-update
  222.8 11.1 %reduce-scatter.2.cloned.1.call-done = bf16[1,512,2432]{2,1,0:T(8,128)(2,1)} async-done(((bf16[2,512,2432]{2,1,0:T(8,128)(2,1)}), bf16[1,512,2432]{2,1,0:T(8,128)(2,1)}) %reduce-scatter.2.cloned.1.call-update) | async-done | bytes 2490384 | tf_op jit(solution)/shard_map/reduce_scatter | solution.py:139
  233.9 4.1 %fusion.27 = f32[512]{0:T(512)S(1)} fusion(f32[512,2432]{1,0:T(8,128)} %copy-done.2, bf16[1,512,2432]{2,1,0:T(8,128)(2,1)} %reduce-scatter.2.cloned.1.call-done, f32[2432]{0:T(1024)S(1)} %get-tuple-element.4), kind=kLoop, calls=%fused_computation.38 | loop fusion | flops 4980224 | bytes 7482880 | tf_op jit(solution)/shard_map/reduce_sum | solution.py:44
  238.0 3.7 %multiply_reduce_fusion.1 = f32[512]{0:T(512)S(1)} fusion(f32[512]{0:T(512)S(1)} %broadcast_multiply_fusion, f32[512,2432]{1,0:T(8,128)} %copy-done.2, bf16[1,512,2432]{2,1,0:T(8,128)(2,1)S(1)} %copy-done.3, f32[2432]{0:T(1024)S(1)} %get-tuple-element.4), kind=kLoop, calls=%fused_computation.19 | loop fusion | flops 7470592 | bytes 7484928 | tf_op jit(solution)/shard_map/reduce_sum | solution.py:45
  241.7 0.0 copy-start.9
  241.8 0.0 copy-start.8
  241.8 0.0 copy-start.1
  241.8 1.3 fusion.28
  243.1 0.4 copy.42
  243.5 0.2 copy.43
  243.7 3.8 %all_to_all.4 = bf16[1,16,8,256]{3,1,0,2:T(8,128)(2,1)S(1)} all-to-all(bf16[1,16,8,256]{3,1,0,2:T(8,128)(2,1)S(1)} %copy.43), channel_id=1, replica_groups=mesh['groups'=2,'width'=8,'guide'=2] {'guide'}, dimensions={2} | all-to-all | bytes 131072 | tf_op jit(solution)/shard_map/all_to_all | solution.py:146
  247.6 2.6 dynamic_update_slice.3
  250.2 1.9 collective-permute-start.3
  252.1 4.6 %collective-permute-done.3 = bf16[16,4,128]{2,1,0:T(4,128)(2,1)S(1)} collective-permute-done((bf16[16,4,128]{2,1,0:T(4,128)(2,1)S(1)}, bf16[16,4,128]{2,1,0:T(4,128)(2,1)S(1)}, u32[]{:S(2)}, u32[]{:S(2)}) %collective-permute-start.3) | collective-permute-done | bytes 16416 | tf_op jit(solution)/shard_map/ppermute | solution.py:17
  256.7 0.1 collective-permute-start.4
  257.5 5.7 %collective-permute-done.4 = bf16[16,4,128]{2,1,0:T(4,128)(2,1)S(1)} collective-permute-done((bf16[16,4,128]{2,1,0:T(4,128)(2,1)S(1)}, bf16[16,4,128]{2,1,0:T(4,128)(2,1)S(1)}, u32[]{:S(2)}, u32[]{:S(2)}) %collective-permute-start.4) | collective-permute-done | bytes 16416 | tf_op jit(solution)/shard_map/ppermute | solution.py:17
  263.2 0.6 fusion.49
  263.8 1.3 collective-permute-start.5
  265.1 1.3 collective-permute-start.6
  266.4 0.0 collective-permute-done.5
  266.5 1.8 collective-permute-done.6
  268.2 0.1 fusion.50
  268.3 1.3 collective-permute-start.7
  269.6 1.3 collective-permute-start.8
  270.9 0.3 collective-permute-done.7
  271.2 0.1 constant_dynamic-update-slice_fusion.8
  271.3 4.1 %collective-permute-done.8 = bf16[16,6,1]{2,1,0:T(8,128)(2,1)S(1)} collective-permute-done((bf16[16,6,1]{2,1,0:T(8,128)(2,1)S(1)}, bf16[16,6,1]{2,1,0:T(8,128)(2,1)S(1)}, u32[]{:S(2)}, u32[]{:S(2)}) %collective-permute-start.8) | collective-permute-done | bytes 224 | tf_op jit(solution)/shard_map/ppermute | solution.py:38
  275.4 0.1 constant_dynamic-update-slice_fusion.6
  275.6 0.1 constant_dynamic-update-slice_fusion.5
  275.7 0.1 constant_dynamic-update-slice_fusion.3
  275.8 0.1 constant_dynamic-update-slice_fusion.2
  276.0 0.1 constant_dynamic-update-slice_fusion
  276.1 1.3 multiply_convert_fusion.6
  (42 shorter events, 0.4 us)
Async XLA Ops:
  7.2 23.3 %copy-start = (bf16[64,2432]{1,0:T(8,128)(2,1)S(1)}, bf16[64,2432]{1,0:T(8,128)(2,1)}, u32[]{:S(2)}) copy-start(bf16[64,2432]{1,0:T(8,128)(2,1)} %param.15) | copy-start | bytes 933892
  7.2 146.5 %all-gather.2.cloned.1.call-start = ((), (), s32[]{:S(2)}) async-start(), calls=%async_computation.2 | async-start | bytes 10506240 | tf_op jit(solution)/shard_map/all_gather | solution.py:127
  7.2 7.6 %copy-start.6 = (f32[16,8,128]{2,1,0:T(8,128)S(1)}, f32[16,8,128]{2,1,0:T(8,128)}, u32[]{:S(2)}) copy-start(f32[16,8,128]{2,1,0:T(8,128)} %param.10) | copy-start | bytes 196612
  7.2 20.3 %copy-start.7 = (f32[1,3,2432]{2,0,1:T(1,128)S(1)}, f32[1,3,2432]{2,0,1:T(1,128)}, u32[]{:S(2)}) copy-start(f32[1,3,2432]{2,0,1:T(1,128)} %param.14) | copy-start | bytes 87556
  14.8 219.1 %reduce-scatter.2.cloned.1.call-start = ((), (), s32[]{:S(2)}) async-start(), calls=%async_computation.3 | async-start | bytes 7471104 | tf_op jit(solution)/shard_map/reduce_scatter | solution.py:139
  14.8 7.7 %collective-permute-start = (bf16[16,8,128]{2,1,0:T(8,128)(2,1)S(1)}, bf16[16,8,128]{2,1,0:T(8,128)(2,1)S(1)}, u32[]{:S(2)}, u32[]{:S(2)}) collective-permute-start(bf16[16,8,128]{2,1,0:T(8,128)(2,1)S(1)} %convert_element_type.86), channel_id=1, source_target_pairs={{0,14},{2,0},{4,2},{6,4},{8,6},{10,8},{12,10},{14,12},{1,15},{3,1}... | collective-permute-start | bytes 98312 | tf_op jit(solution)/shard_map/ppermute | solution.py:17
  22.5 7.2 %collective-permute-start.1 = (bf16[16,8,128]{2,1,0:T(8,128)(2,1)S(1)}, bf16[16,8,128]{2,1,0:T(8,128)(2,1)S(1)}, u32[]{:S(2)}, u32[]{:S(2)}) collective-permute-start(bf16[16,8,128]{2,1,0:T(8,128)(2,1)S(1)} %collective-permute-done), channel_id=1, source_target_pairs={{0,14},{2,0},{4,2},{6,4},{8,6},{10,8},{12,10},{14,12},{1,15},{3,1}... | collective-permute-start | bytes 98312 | tf_op jit(solution)/shard_map/ppermute | solution.py:17
  31.4 2.2 copy-start.2
  33.6 133.3 %collective-permute-start.2 = (bf16[512,2432]{1,0:T(8,128)(2,1)S(1)}, bf16[512,2432]{1,0:T(8,128)(2,1)}, u32[]{:S(2)}, u32[]{:S(2)}) collective-permute-start(bf16[512,2432]{1,0:T(8,128)(2,1)S(1)} %add_convert_fusion), channel_id=1, source_target_pairs={{0,1},{1,0},{2,3},{3,2},{4,5},{5,4},{6,7},{7,6},{8,9},{9,8},{10,11... | collective-permute-start | bytes 7471112 | tf_op jit(solution)/shard_map/ppermute | solution.py:27
  189.9 3.1 %copy-start.4 = (f32[2,512,3,10,64]{1,4,3,2,0:T(8,128)}, f32[2,512,3,10,64]{1,4,3,2,0:T(8,128)S(1)}, u32[]{:S(2)}) copy-start(f32[2,512,3,10,64]{1,4,3,2,0:T(8,128)S(1)} %fusion.7) | copy-start | bytes 23592964
  193.9 22.8 %slice-start.2 = ((s8[6225920]{0:T(1024)(128)(4,1)}), s8[2031616]{0:T(1024)(128)(4,1)S(1)}, s32[]{:S(2)}) async-start(s8[6225920]{0:T(1024)(128)(4,1)} %bitcast.162), calls=%async_computation.6 | async-start | bytes 4063232
  206.8 9.9 %slice-start.3 = ((s8[6225920]{0:T(1024)(128)(4,1)}), s8[4194304]{0:T(1024)(128)(4,1)S(1)}, s32[]{:S(2)}) async-start(s8[6225920]{0:T(1024)(128)(4,1)} %bitcast.162), calls=%async_computation.7 | async-start | bytes 8388608
  222.7 19.0 %slice-start = ((s8[4980736]{0:T(1024)(128)(4,1)}), s8[786432]{0:T(1024)(128)(4,1)S(1)}, s32[]{:S(2)}) async-start(s8[4980736]{0:T(1024)(128)(4,1)} %bitcast.151), calls=%async_computation.4 | async-start | bytes 1572864
  233.9 4.1 %copy-start.3 = (bf16[1,512,2432]{2,1,0:T(8,128)(2,1)S(1)}, bf16[1,512,2432]{2,1,0:T(8,128)(2,1)}, u32[]{:S(2)}) copy-start(bf16[1,512,2432]{2,1,0:T(8,128)(2,1)} %reduce-scatter.2.cloned.1.call-done) | copy-start | bytes 7471108
  233.9 7.8 %slice-start.1 = ((s8[4980736]{0:T(1024)(128)(4,1)}), s8[4194304]{0:T(1024)(128)(4,1)S(1)}, s32[]{:S(2)}) async-start(s8[4980736]{0:T(1024)(128)(4,1)} %bitcast.151), calls=%async_computation.5 | async-start | bytes 8388608
  238.0 3.8 %copy-start.5 = (bf16[2432,64]{0,1:T(8,128)(2,1)S(1)}, bf16[2432,64]{0,1:T(8,128)(2,1)}, u32[]{:S(2)}) copy-start(bf16[2432,64]{0,1:T(8,128)(2,1)} %param.18) | copy-start | bytes 933892
  241.7 15.7 %copy-start.9 = (s32[128]{0:T(128)S(1)}, s32[128]{0:T(128)}, u32[]{:S(2)}) copy-start(s32[128]{0:T(128)} %param.12) | copy-start | bytes 1540
  241.8 34.4 %copy-start.8 = (bf16[144,512]{1,0:T(8,128)(2,1)S(1)}, bf16[144,512]{1,0:T(8,128)(2,1)}, u32[]{:S(2)}) copy-start(bf16[144,512]{1,0:T(8,128)(2,1)} %param.19) | copy-start | bytes 442372
  241.8 35.7 %copy-start.1 = (bf16[64,2432]{1,0:T(8,128)(2,1)S(1)}, bf16[64,2432]{1,0:T(8,128)(2,1)}, u32[]{:S(2)}) copy-start(bf16[64,2432]{1,0:T(8,128)(2,1)} %param.15) | copy-start | bytes 933892
  250.2 6.5 %collective-permute-start.3 = (bf16[16,4,128]{2,1,0:T(4,128)(2,1)S(1)}, bf16[16,4,128]{2,1,0:T(4,128)(2,1)S(1)}, u32[]{:S(2)}, u32[]{:S(2)}) collective-permute-start(bf16[16,4,128]{2,1,0:T(4,128)(2,1)S(1)} %slice.166), channel_id=1, source_target_pairs={{0,2},{2,4},{4,6},{6,8},{8,10},{10,12},{12,14},{14,0},{1,3},{3,5},... | collective-permute-start | bytes 49160 | tf_op jit(solution)/shard_map/ppermute | solution.py:17
  256.7 6.5 %collective-permute-start.4 = (bf16[16,4,128]{2,1,0:T(4,128)(2,1)S(1)}, bf16[16,4,128]{2,1,0:T(4,128)(2,1)S(1)}, u32[]{:S(2)}, u32[]{:S(2)}) collective-permute-start(bf16[16,4,128]{2,1,0:T(4,128)(2,1)S(1)} %fusion.40), channel_id=1, source_target_pairs={{0,2},{2,4},{4,6},{6,8},{8,10},{10,12},{12,14},{14,0},{1,3},{3,5},... | collective-permute-start | bytes 49160 | tf_op jit(solution)/shard_map/ppermute | solution.py:17
  263.8 2.6 collective-permute-start.5
  265.1 3.1 %collective-permute-start.6 = (bf16[16,1,128]{2,1,0:T(2,128)(2,1)S(1)}, bf16[16,1,128]{2,1,0:T(2,128)(2,1)S(1)}, u32[]{:S(2)}, u32[]{:S(2)}) collective-permute-start(bf16[16,1,128]{2,1,0:T(2,128)(2,1)S(1)} %get-tuple-element.14), channel_id=1, source_target_pairs={{1,0},{3,2},{5,4},{7,6},{9,8},{11,10},{13,12},{15,14},{17,16},{19,... | collective-permute-start | bytes 12296 | tf_op jit(solution)/shard_map/ppermute | solution.py:38
  268.3 2.9 %collective-permute-start.7 = (bf16[16,6,1]{2,1,0:T(8,128)(2,1)S(1)}, bf16[16,6,1]{2,1,0:T(8,128)(2,1)S(1)}, u32[]{:S(2)}, u32[]{:S(2)}) collective-permute-start(bf16[16,6,1]{2,1,0:T(8,128)(2,1)S(1)} %get-tuple-element.12), channel_id=1, source_target_pairs={{0,2},{2,4},{4,6},{6,8},{8,10},{10,12},{12,14},{1,3},{3,5},{5,7},{... | collective-permute-start | bytes 584 | tf_op jit(solution)/shard_map/ppermute | solution.py:35
  269.6 5.8 %collective-permute-start.8 = (bf16[16,6,1]{2,1,0:T(8,128)(2,1)S(1)}, bf16[16,6,1]{2,1,0:T(8,128)(2,1)S(1)}, u32[]{:S(2)}, u32[]{:S(2)}) collective-permute-start(bf16[16,6,1]{2,1,0:T(8,128)(2,1)S(1)} %get-tuple-element.11), channel_id=1, source_target_pairs={{2,0},{4,2},{6,4},{8,6},{10,8},{12,10},{14,12},{3,1},{5,3},{7,5},{... | collective-permute-start | bytes 584 | tf_op jit(solution)/shard_map/ppermute | solution.py:38
Sparse Core Ops, SparseCore 0:
  14.9 138.7 all-gather.1
  222.9 10.9 reduce-scatter.1
where the time goes:
time: 285 us; the launch traced here: 284 us
  waiting for transfers between devices  146 us (51%)
  matrix products  55.3 us (19%)
  local copies, waits for them, and re-layouts  28.5 us (10%)
  starting transfers between devices  18.3 us (6%)
  other arithmetic  16.8 us (6%)
  between operations  15.8 us (6%)
  blocking collectives  3.79 us (1%)
    all_gather x1, waiting for transfers between devices, shards(): lax.all_gather(weight_half, 'width', axis=0, tiled=True)  115 us
    dot_general x1, matrix products, shards(): jnp.dot(both_rows, lax.all_gather(weight_half, 'width', axis=0, tiled=Tru...  23 us
    ppermute x4, waiting for transfers between devices, from_behind(): return lax.ppermute(x, axis, [(i, (i + by) % peers) for i in range(peers)])  13.3 us
    dot_general x1, local copies, waits for them, and re-layouts, shards(): jnp.dot(both_rows, lax.all_gather(weight_half, 'width', axis=0, tiled=Tru...  13.3 us
    ppermute x4, starting transfers between devices, from_behind(): return lax.ppermute(x, axis, [(i, (i + by) % peers) for i in range(peers)])  13.1 us
    sub x1, matrix products, attend(): weights = jax.nn.softmax(scores, axis=-1).astype(jnp.bfloat16)  13 us
    reduce_scatter x1, waiting for transfers between devices, shards(): lax.psum_scatter(partial_value.astype(jnp.bfloat16), 'guide', scatter_dim...  11.1 us
    dot_general x1, matrix products, attend(): jnp.einsum('bhqk,bkhe->bqhe', weights, value_rows, preferred_element_type...  9.84 us
  transfers between devices with their start and end apart: 11, of which 9 were waited for; matrix products, arithmetic and copies ran while one was open for 8% of the time, Pallas kernels for 0%

commit v1 on v0

--- a/solution.py
+++ b/solution.py
@@ -3,7 +3,6 @@
 from jax import lax
 from jax.sharding import PartitionSpec as P
 
-HEADS = 20
 HEAD = 64
 STEPS = 28
 
@@ -85,6 +84,24 @@
     return jax.nn.silu(summed).astype(jnp.bfloat16).reshape(height, breadth, w_dec.shape[1])
 
 
+def halves(values):
+    high = lax.reduce_precision(values, 8, 7)
+    return high.astype(jnp.bfloat16), (values - high).astype(jnp.bfloat16)
+
+
+def fold(modulation, w_patch, w_qkv, place):
+    patch = w_patch.astype(jnp.float32)
+    patch = patch - jnp.mean(patch, axis=1, keepdims=True)
+    rows = jnp.concatenate([patch * (1.0 + modulation[1]), modulation[0:1]], axis=0)
+    depth = w_qkv.shape[0]
+    rows = lax.dynamic_slice_in_dim(rows, place * depth, depth, 1)
+    high, low = halves(rows)
+    both = jnp.dot(
+        jnp.concatenate([high, low], axis=0), w_qkv, preferred_element_type=jnp.float32
+    )
+    return both[: rows.shape[0]] + both[rows.shape[0] :]
+
+
 def fetch_next(block):
     return from_behind(block, "width", -1)
 
@@ -110,35 +127,25 @@
     patches = patchify(window)
     token_count = patches.shape[0]
     hidden = jnp.dot(patches, w_patch, preferred_element_type=jnp.float32)
-    modulated = (layer_norm(hidden) * (1.0 + modulation[1]) + modulation[0]).astype(jnp.bfloat16)
-    partner = from_partner(modulated, "guide", 0)
-    both_rows = jnp.where(
-        guide_at == 0, jnp.stack([modulated, partner]), jnp.stack([partner, modulated])
-    )
-    both_rows = both_rows.reshape(2 * token_count, modulated.shape[1])
-    head_share = HEADS // 2
-    shard_rows = w_qkv.shape[0]
-    weight_half = lax.dynamic_slice_in_dim(
-        w_qkv.reshape(shard_rows, 3, HEADS, HEAD), guide_at * head_share, head_share, 2
-    )
-    weight_half = weight_half.reshape(shard_rows, 3 * head_share * HEAD)
+    centered = hidden - jnp.mean(hidden, axis=-1, keepdims=True)
+    rstd = lax.rsqrt(jnp.mean(centered * centered, axis=-1, keepdims=True) + epsilon)
+    heads = w_qkv.shape[1] // (3 * HEAD)
+    folded = lax.psum(fold(modulation, w_patch, w_qkv, place), "width")
+    patch_rows = w_patch.shape[0]
+    high, low = halves(folded[:patch_rows])
     projected = jnp.dot(
-        both_rows,
-        lax.all_gather(weight_half, "width", axis=0, tiled=True),
+        jnp.concatenate([patches, patches], axis=1),
+        jnp.concatenate([high, low], axis=0),
         preferred_element_type=jnp.float32,
     )
-    projected = projected.reshape(2, token_count, 3, head_share, HEAD)
-    queries = head_norm(projected[:, :, 0]).astype(jnp.bfloat16)
-    key_rows = head_norm(projected[:, :, 1]).astype(jnp.bfloat16)
-    value_rows = projected[:, :, 2].astype(jnp.bfloat16)
-    attended = attend(queries, key_rows, value_rows).reshape(2 * token_count, head_share * HEAD)
-    out_rows = lax.dynamic_slice_in_dim(w_out, guide_at * head_share * HEAD, head_share * HEAD, 0)
-    partial_value = jnp.dot(attended, out_rows, preferred_element_type=jnp.float32).reshape(
-        2, token_count, w_out.shape[1]
-    )
-    mixed_out = lax.psum_scatter(
-        partial_value.astype(jnp.bfloat16), "guide", scatter_dimension=0, tiled=True
-    ).astype(jnp.float32)[0]
+    projected = projected * rstd + folded[patch_rows : patch_rows + 1]
+    projected = projected.reshape(token_count, 3, heads, HEAD)
+    queries = head_norm(projected[:, 0]).astype(jnp.bfloat16)
+    key_rows = head_norm(projected[:, 1]).astype(jnp.bfloat16)
+    value_rows = projected[:, 2].astype(jnp.bfloat16)
+    attended = attend(queries[None], key_rows[None], value_rows[None])[0]
+    attended = attended.reshape(token_count, heads * HEAD)
+    mixed_out = jnp.dot(attended, w_out, preferred_element_type=jnp.float32)
     residual = hidden + modulation[2] * mixed_out
     final_in = layer_norm(residual).astype(jnp.bfloat16)
     result = jnp.dot(final_in, w_final, preferred_element_type=jnp.float32)

time: 285 us -> 191 us (0.67)
  waiting for transfers between devices: 146 us -> 88.3 us
  matrix products: 55.3 us -> 37.3 us
  local copies, waits for them, and re-layouts: 28.5 us -> 16.5 us
  other arithmetic: 16.8 us -> 12.9 us
  starting transfers between devices: 18.3 us -> 15.4 us
    all_gather x1 -> x0, waiting for transfers between devices: 115 us -> none  [shards(): lax.all_gather(weight_half, 'width', axis=0, tiled=True)]
    psum x0 -> x1, waiting for transfers between devices: none -> 71.3 us  [shards(): folded = lax.psum(fold(modulation, w_patch, w_qkv, place), 'width')]
    dot_general x2 -> x3, matrix products: 29 us -> 11.3 us  [the longest x1 6.33 us: shards(): mixed_out = jnp.dot(attended, w_out, preferred_element_type=jnp.float32)]
    dot_general x1 -> x0, local copies, waits for them, and re-layouts: 13.3 us -> none  [shards(): jnp.dot(both_rows, lax.all_gather(weight_half, 'width', axis=0, tiled=Tru...]
    reduce_scatter x1 -> x0, waiting for transfers between devices: 11.1 us -> none  [shards(): lax.psum_scatter(partial_value.astype(jnp.bfloat16), 'guide', scatter_dim...]
    add x0 -> x1, local copies, waits for them, and re-layouts: none -> 9.07 us  [shards(): projected = projected * rstd + folded[patch_rows:patch_rows + 1]]
    unnamed x30 -> x20, local copies, waits for them, and re-layouts: 7.43 us -> 2.51 us
    another operation x1 -> x0, other arithmetic: 4.86 us -> none  [shards(): jnp.stack([modulated, partner])]
  transfers between devices with their start and end apart: 11 -> 9, of which waited for: 9 -> 6; matrix products, arithmetic and copies ran while one was open for 8% -> 4% of each run, Pallas kernels for 0% -> 0%
where the time goes in v1:
time: 191 us; the launch traced here: 190 us
  waiting for transfers between devices  88.3 us (46%)
  matrix products  37.3 us (20%)
  local copies, waits for them, and re-layouts  16.5 us (9%)
  between operations  15.8 us (8%)
  starting transfers between devices  15.4 us (8%)
  other arithmetic  12.9 us (7%)
  blocking collectives  3.79 us (2%)
    psum x1, waiting for transfers between devices, shards(): folded = lax.psum(fold(modulation, w_patch, w_qkv, place), 'width')  71.3 us
    sub x1, matrix products, attend(): weights = jax.nn.softmax(scores, axis=-1).astype(jnp.bfloat16)  12.8 us
    ppermute x4, waiting for transfers between devices, from_behind(): return lax.ppermute(x, axis, [(i, (i + by) % peers) for i in range(peers)])  10.8 us
    ppermute x4, starting transfers between devices, from_behind(): return lax.ppermute(x, axis, [(i, (i + by) % peers) for i in range(peers)])  10.2 us
    dot_general x1, matrix products, attend(): jnp.einsum('bhqk,bkhe->bqhe', weights, value_rows, preferred_element_type...  9.86 us
    add x1, local copies, waits for them, and re-layouts, shards(): projected = projected * rstd + folded[patch_rows:patch_rows + 1]  9.07 us
    dot_general x1, matrix products, shards(): mixed_out = jnp.dot(attended, w_out, preferred_element_type=jnp.float32)  6.33 us
    ppermute x2, waiting for transfers between devices, extended(): lax.ppermute(lax.slice_in_dim(block, 0, width, axis=dim), axis, backward)  5.84 us
  transfers between devices with their start and end apart: 9, of which 6 were waited for; matrix products, arithmetic and copies ran while one was open for 4% of the time, Pallas kernels for 0%

profile of v1, /device:TPU:0, one launch (start us, length us, event | category | flops | bytes accessed | tf_op | source)
XLA Modules:
  0.0 190.0 jit_solution(14800418378556094931)
XLA Ops:
  7.2 0.0 copy-start
  7.2 0.0 all-reduce.2.cloned.1.call-start
  7.2 1.0 convert_element_type.102
  8.2 6.0 %collective-permute-start = (bf16[16,8,128]{2,1,0:T(8,128)(2,1)S(1)}, bf16[16,8,128]{2,1,0:T(8,128)(2,1)S(1)}, u32[]{:S(2)}, u32[]{:S(2)}) collective-permute-start(bf16[16,8,128]{2,1,0:T(8,128)(2,1)S(1)} %convert_element_type.102), channel_id=1, source_target_pairs={{0,14},{2,0},{4,2},{6,4},{8,6},{10,8},{12,10},{14,12},{1,15},{3,1}... | collective-permute-start | bytes 98312 | tf_op jit(solution)/shard_map/ppermute | solution.py:16
  14.3 0.8 slice_reduce_fusion.1
  15.0 1.1 convert_reduce_fusion
  16.2 1.1 fusion.20
  17.3 0.1 reduce-precision_convert_fusion.1
  17.4 0.0 copy-done
  17.4 0.0 copy-start.2
  17.4 0.7 fusion.29
  18.1 0.0 collective-permute-done
  18.1 2.7 %collective-permute-start.1 = (bf16[16,8,128]{2,1,0:T(8,128)(2,1)S(1)}, bf16[16,8,128]{2,1,0:T(8,128)(2,1)S(1)}, u32[]{:S(2)}, u32[]{:S(2)}) collective-permute-start(bf16[16,8,128]{2,1,0:T(8,128)(2,1)S(1)} %collective-permute-done), channel_id=1, source_target_pairs={{0,14},{2,0},{4,2},{6,4},{8,6},{10,8},{12,10},{14,12},{1,15},{3,1}... | collective-permute-start | bytes 98312 | tf_op jit(solution)/shard_map/ppermute | solution.py:16
  20.9 1.2 slice_add_fusion
  22.0 0.0 all-reduce.2.cloned.1.call-update
  22.7 0.0 collective-permute-done.1
  22.7 0.1 fusion.34
  22.9 0.3 copy.24
  23.1 0.4 copy.25
  23.6 0.9 fusion.51
  24.5 2.2 %copy-done.1 = f32[512,2432]{1,0:T(8,128)} copy-done((f32[512,2432]{1,0:T(8,128)}, f32[512,2432]{1,0:T(8,128)S(1)}, u32[]{:S(2)}) %copy-start.1) | copy-done | bytes 4980760
  26.7 0.6 multiply_reduce_fusion.2
  27.3 71.3 %all-reduce.2.cloned.1.call-done = f32[65,3840]{1,0:T(8,128)} async-done(((f32[65,3840]{1,0:T(8,128)}), f32[65,3840]{1,0:T(8,128)}) %all-reduce.2.cloned.1.call-update) | async-done | bytes 998416 | tf_op jit(solution)/shard_map/psum | solution.py:133
  98.6 1.3 reduce-precision_convert_fusion
  99.9 0.9 slice_reduce_fusion
  100.9 4.3 %multiply_add_fusion = f32[512,3840]{1,0:T(8,128)} fusion(f32[3840]{0:T(1024)S(1)} %slice_reduce_fusion, f32[512]{0:T(512)S(1)} %add_rsqrt_fusion.3, bf16[64,3840]{1,0:T(8,128)(2,1)S(1)} %get-tuple-element.9, bf16[64,3840]{1,0:T(8,128)(2,1)S(1)} %get-tuple-element.8, bf16[512,64]{0,1:T(8,128)(2,1)S(1)} %bitcast.139), kind=kOutput, calls=%fused_computation.7 | convolution fusion | flops 509476864 | bytes 8930304 | tf_op jit(solution)/shard_map/dot_general | solution.py:136
  105.2 9.1 %copy.26 = f32[512,3840]{0,1:T(8,128)} copy(f32[512,3840]{1,0:T(8,128)} %multiply_add_fusion) | data formatting | bytes 15728640 | tf_op jit(solution)/shard_map/add | solution.py:141
  114.2 3.3 %multiply_reduce_fusion.3 = (f32[512,20]{0,1:T(8,128)S(1)}, f32[512,20]{0,1:T(8,128)S(1)}) fusion(f32[512,3,20,64]{0,3,2,1:T(8,128)} %bitcast.131), kind=kLoop, calls=%fused_computation.18 | loop fusion | flops 2600960 | bytes 5324800 | tf_op jit(solution)/shard_map/reduce_sum | solution.py:49
  117.6 0.0 slice-start
  117.6 12.8 %fusion.52 = (f32[20,512]{1,0:T(8,128)S(1)}, f32[20,512,512]{1,2,0:T(8,128)}) fusion(f32[512,3,20,64]{0,3,2,1:T(8,128)} %bitcast.132, f32[512,20]{0,1:T(8,128)S(1)} %get-tuple-element.26, f32[512,20]{0,1:T(8,128)S(1)} %get-tuple-element.25), kind=kOutput, calls=%fused_computation.118 | convolution fusion | flops 689439232 | bytes 26337280 | tf_op jit(solution)/shard_map/sub | solution.py:66
  130.4 9.9 %fusion.12 = bf16[20,64,512]{2,1,0:T(8,128)(2,1)S(1)} fusion(f32[20,512,512]{1,2,0:T(8,128)} %get-tuple-element.22, f32[20,512]{1,0:T(8,128)S(1)} %get-tuple-element.21, f32[512,3,20,64]{0,3,2,1:T(8,128)} %bitcast.133), kind=kOutput, calls=%fused_computation.24 | convolution fusion | flops 682229760 | bytes 23633920 | tf_op jit(solution)/shard_map/bhqk,bkhe->bqhe/dot_general | solution.py:67
  140.3 6.3 %fusion.53 = (f32[512]{0:T(512)S(1)}, f32[512,2432]{1,0:T(8,128)S(1)}) fusion(f32[512,2432]{1,0:T(8,128)S(1)} %bitcast.130, bf16[512,1280]{0,1:T(8,128)(2,1)S(1)} %bitcast.136, bf16[1280,2432]{1,0:T(8,128)(2,1)} %param.17, f32[2432]{0:T(1024)S(1)} %get-tuple-element.4), kind=kOutput, calls=%fused_computation.119 | convolution fusion | flops 3191406080 | bytes 17509888 | tf_op jit(solution)/shard_map/dot_general | solution.py:148
  146.6 0.0 copy-start.3
  146.6 0.6 multiply_reduce_fusion.1
  147.3 0.0 copy-start.4
  147.3 0.0 copy-start.5
  147.3 0.3 copy-done.3
  147.6 1.1 fusion.15
  148.7 0.4 copy.28
  149.2 0.2 copy.29
  149.3 3.8 %all_to_all.4 = bf16[1,16,8,256]{3,1,0,2:T(8,128)(2,1)S(1)} all-to-all(bf16[1,16,8,256]{3,1,0,2:T(8,128)(2,1)S(1)} %copy.29), channel_id=1, replica_groups=mesh['groups'=2,'width'=8,'guide'=2] {'guide'}, dimensions={2} | all-to-all | bytes 131072 | tf_op jit(solution)/shard_map/all_to_all | solution.py:153
  153.3 2.6 %dynamic_update_slice.3 = f32[16,4,384]{2,1,0:T(4,128)S(1)} dynamic-update-slice(f32[16,4,384]{2,1,0:T(4,128)S(1)} %broadcast_in_dim.2, f32[16,4,256]{2,1,0:T(4,128)S(1)} %copy.32, s32[]{:T(128)} %constant.20.clone.1, s32[]{:T(128)} %constant.20.clone.1, s32[]{:T(128)S(6)} %select_n.11) | dynamic-update-slice | bytes 131076 | tf_op jit(solution)/shard_map/dynamic_update_slice | solution.py:158
  155.9 1.4 collective-permute-start.2
  157.2 5.1 %collective-permute-done.2 = bf16[16,4,128]{2,1,0:T(4,128)(2,1)S(1)} collective-permute-done((bf16[16,4,128]{2,1,0:T(4,128)(2,1)S(1)}, bf16[16,4,128]{2,1,0:T(4,128)(2,1)S(1)}, u32[]{:S(2)}, u32[]{:S(2)}) %collective-permute-start.2) | collective-permute-done | bytes 16416 | tf_op jit(solution)/shard_map/ppermute | solution.py:16
  162.4 0.1 collective-permute-start.3
  163.1 0.0 copy-done.6
  163.2 5.7 %collective-permute-done.3 = bf16[16,4,128]{2,1,0:T(4,128)(2,1)S(1)} collective-permute-done((bf16[16,4,128]{2,1,0:T(4,128)(2,1)S(1)}, bf16[16,4,128]{2,1,0:T(4,128)(2,1)S(1)}, u32[]{:S(2)}, u32[]{:S(2)}) %collective-permute-start.3) | collective-permute-done | bytes 16416 | tf_op jit(solution)/shard_map/ppermute | solution.py:16
  168.9 0.6 fusion.48
  169.5 1.3 collective-permute-start.4
  170.8 1.3 collective-permute-start.5
  172.1 0.0 collective-permute-done.4
  172.1 1.8 collective-permute-done.5
  173.9 0.1 fusion.49
  174.0 1.3 collective-permute-start.6
  175.3 1.3 collective-permute-start.7
  176.6 0.3 collective-permute-done.6
  176.9 0.1 constant_dynamic-update-slice_fusion.8
  177.0 4.1 %collective-permute-done.7 = bf16[16,6,1]{2,1,0:T(8,128)(2,1)S(1)} collective-permute-done((bf16[16,6,1]{2,1,0:T(8,128)(2,1)S(1)}, bf16[16,6,1]{2,1,0:T(8,128)(2,1)S(1)}, u32[]{:S(2)}, u32[]{:S(2)}) %collective-permute-start.7) | collective-permute-done | bytes 224 | tf_op jit(solution)/shard_map/ppermute | solution.py:37
  181.1 0.1 constant_dynamic-update-slice_fusion.6
  181.2 0.1 constant_dynamic-update-slice_fusion.5
  181.4 0.1 constant_dynamic-update-slice_fusion.3
  181.5 0.1 constant_dynamic-update-slice_fusion.2
  181.7 0.1 constant_dynamic-update-slice_fusion
  181.8 1.3 multiply_convert_fusion.6
  (29 shorter events, 0.3 us)
Async XLA Ops:
  7.2 10.3 %copy-start = (bf16[304,3840]{1,0:T(8,128)(2,1)S(1)}, bf16[304,3840]{1,0:T(8,128)(2,1)}, u32[]{:S(2)}) copy-start(bf16[304,3840]{1,0:T(8,128)(2,1)} %param.16) | copy-start | bytes 7004164
  7.2 91.4 %all-reduce.2.cloned.1.call-start = ((), (), s32[]{:S(2)}) async-start(), calls=%async_computation.1 | async-start | bytes 2211840 | tf_op jit(solution)/shard_map/psum | solution.py:133
  8.2 9.9 %collective-permute-start = (bf16[16,8,128]{2,1,0:T(8,128)(2,1)S(1)}, bf16[16,8,128]{2,1,0:T(8,128)(2,1)S(1)}, u32[]{:S(2)}, u32[]{:S(2)}) collective-permute-start(bf16[16,8,128]{2,1,0:T(8,128)(2,1)S(1)} %convert_element_type.102), channel_id=1, source_target_pairs={{0,14},{2,0},{4,2},{6,4},{8,6},{10,8},{12,10},{14,12},{1,15},{3,1}... | collective-permute-start | bytes 98312 | tf_op jit(solution)/shard_map/ppermute | solution.py:16
  17.4 6.1 %copy-start.2 = (bf16[64,2432]{1,0:T(8,128)(2,1)S(1)}, bf16[64,2432]{1,0:T(8,128)(2,1)}, u32[]{:S(2)}) copy-start(bf16[64,2432]{1,0:T(8,128)(2,1)} %param.15) | copy-start | bytes 933892
  18.1 4.6 %collective-permute-start.1 = (bf16[16,8,128]{2,1,0:T(8,128)(2,1)S(1)}, bf16[16,8,128]{2,1,0:T(8,128)(2,1)S(1)}, u32[]{:S(2)}, u32[]{:S(2)}) collective-permute-start(bf16[16,8,128]{2,1,0:T(8,128)(2,1)S(1)} %collective-permute-done), channel_id=1, source_target_pairs={{0,14},{2,0},{4,2},{6,4},{8,6},{10,8},{12,10},{14,12},{1,15},{3,1}... | collective-permute-start | bytes 98312 | tf_op jit(solution)/shard_map/ppermute | solution.py:16
  24.5 2.2 %copy-start.1 = (f32[512,2432]{1,0:T(8,128)}, f32[512,2432]{1,0:T(8,128)S(1)}, u32[]{:S(2)}) copy-start(f32[512,2432]{1,0:T(8,128)S(1)} %get-tuple-element.20) | copy-start | bytes 14942212
  117.6 22.7 %slice-start = ((s8[4980736]{0:T(1024)(128)(4,1)}), s8[786432]{0:T(1024)(128)(4,1)S(1)}, s32[]{:S(2)}) async-start(s8[4980736]{0:T(1024)(128)(4,1)} %bitcast.129), calls=%async_computation.2 | async-start | bytes 1572864
  130.4 9.9 %slice-start.1 = ((s8[4980736]{0:T(1024)(128)(4,1)}), s8[4194304]{0:T(1024)(128)(4,1)S(1)}, s32[]{:S(2)}) async-start(s8[4980736]{0:T(1024)(128)(4,1)} %bitcast.129), calls=%async_computation.3 | async-start | bytes 8388608
  146.6 1.0 copy-start.3
  147.3 15.8 %copy-start.6 = (s32[128]{0:T(128)S(1)}, s32[128]{0:T(128)}, u32[]{:S(2)}) copy-start(s32[128]{0:T(128)} %param.12) | copy-start | bytes 1540
  147.3 21.6 %copy-start.4 = (f32[16,8,128]{2,1,0:T(8,128)S(1)}, f32[16,8,128]{2,1,0:T(8,128)}, u32[]{:S(2)}) copy-start(f32[16,8,128]{2,1,0:T(8,128)} %param.10) | copy-start | bytes 196612
  147.3 34.5 %copy-start.5 = (bf16[144,512]{1,0:T(8,128)(2,1)S(1)}, bf16[144,512]{1,0:T(8,128)(2,1)}, u32[]{:S(2)}) copy-start(bf16[144,512]{1,0:T(8,128)(2,1)} %param.19) | copy-start | bytes 442372
  155.9 6.5 %collective-permute-start.2 = (bf16[16,4,128]{2,1,0:T(4,128)(2,1)S(1)}, bf16[16,4,128]{2,1,0:T(4,128)(2,1)S(1)}, u32[]{:S(2)}, u32[]{:S(2)}) collective-permute-start(bf16[16,4,128]{2,1,0:T(4,128)(2,1)S(1)} %slice.194), channel_id=1, source_target_pairs={{0,2},{2,4},{4,6},{6,8},{8,10},{10,12},{12,14},{14,0},{1,3},{3,5},... | collective-permute-start | bytes 49160 | tf_op jit(solution)/shard_map/ppermute | solution.py:16
  162.4 6.5 %collective-permute-start.3 = (bf16[16,4,128]{2,1,0:T(4,128)(2,1)S(1)}, bf16[16,4,128]{2,1,0:T(4,128)(2,1)S(1)}, u32[]{:S(2)}, u32[]{:S(2)}) collective-permute-start(bf16[16,4,128]{2,1,0:T(4,128)(2,1)S(1)} %fusion.38), channel_id=1, source_target_pairs={{0,2},{2,4},{4,6},{6,8},{8,10},{10,12},{12,14},{14,0},{1,3},{3,5},... | collective-permute-start | bytes 49160 | tf_op jit(solution)/shard_map/ppermute | solution.py:16
  169.5 2.6 %collective-permute-start.4 = (bf16[16,1,128]{2,1,0:T(2,128)(2,1)S(1)}, bf16[16,1,128]{2,1,0:T(2,128)(2,1)S(1)}, u32[]{:S(2)}, u32[]{:S(2)}) collective-permute-start(bf16[16,1,128]{2,1,0:T(2,128)(2,1)S(1)} %get-tuple-element.17), channel_id=1, source_target_pairs={{0,1},{2,3},{4,5},{6,7},{8,9},{10,11},{12,13},{14,15},{16,17},{18,... | collective-permute-start | bytes 12296 | tf_op jit(solution)/shard_map/ppermute | solution.py:34
  170.8 3.1 %collective-permute-start.5 = (bf16[16,1,128]{2,1,0:T(2,128)(2,1)S(1)}, bf16[16,1,128]{2,1,0:T(2,128)(2,1)S(1)}, u32[]{:S(2)}, u32[]{:S(2)}) collective-permute-start(bf16[16,1,128]{2,1,0:T(2,128)(2,1)S(1)} %get-tuple-element.18), channel_id=1, source_target_pairs={{1,0},{3,2},{5,4},{7,6},{9,8},{11,10},{13,12},{15,14},{17,16},{19,... | collective-permute-start | bytes 12296 | tf_op jit(solution)/shard_map/ppermute | solution.py:37
  174.0 2.9 %collective-permute-start.6 = (bf16[16,6,1]{2,1,0:T(8,128)(2,1)S(1)}, bf16[16,6,1]{2,1,0:T(8,128)(2,1)S(1)}, u32[]{:S(2)}, u32[]{:S(2)}) collective-permute-start(bf16[16,6,1]{2,1,0:T(8,128)(2,1)S(1)} %get-tuple-element.15), channel_id=1, source_target_pairs={{0,2},{2,4},{4,6},{6,8},{8,10},{10,12},{12,14},{1,3},{3,5},{5,7},{... | collective-permute-start | bytes 584 | tf_op jit(solution)/shard_map/ppermute | solution.py:34
  175.3 5.8 %collective-permute-start.7 = (bf16[16,6,1]{2,1,0:T(8,128)(2,1)S(1)}, bf16[16,6,1]{2,1,0:T(8,128)(2,1)S(1)}, u32[]{:S(2)}, u32[]{:S(2)}) collective-permute-start(bf16[16,6,1]{2,1,0:T(8,128)(2,1)S(1)} %get-tuple-element.14), channel_id=1, source_target_pairs={{2,0},{4,2},{6,4},{8,6},{10,8},{12,10},{14,12},{3,1},{5,3},{7,5},{... | collective-permute-start | bytes 584 | tf_op jit(solution)/shard_map/ppermute | solution.py:37
Sparse Core Ops, SparseCore 0:
  22.2 76.3 all-reduce.1

commit v2 on v0

v2 whole, which is shorter than its diff:
```python
import functools
import math

import jax
import jax.numpy as jnp
from jax import lax
from jax.experimental import pallas as pl
from jax.experimental.pallas import tpu as pltpu
from jax.sharding import PartitionSpec as P

HEAD = 64
STEPS = 28
LANES = 128
MESH = pl.DeviceIdType.MESH

guidance = 4.0
epsilon = 1e-06


def halves(values):
    high = lax.reduce_precision(values, 8, 7)
    return high.astype(jnp.bfloat16), (values - high).astype(jnp.bfloat16)


def fold_rows(modulation, w_patch, depth, place):
    patch = w_patch.astype(jnp.float32)
    means = jnp.mean(patch, axis=1, keepdims=True)
    part = lax.dynamic_slice_in_dim(w_patch, place * depth, depth, 1).astype(jnp.float32)
    mod = lax.dynamic_slice_in_dim(modulation, place * depth, depth, 1)
    rows = jnp.concatenate([(part - means) * (1.0 + mod[1]), mod[0:1]], axis=0)
    spare = -rows.shape[0] % 16
    rows = jnp.pad(rows, ((0, spare), (0, 0)))
    return jnp.concatenate(halves(rows), axis=0)


def at(groups, width):
    return {"groups": groups, "width": width}


def gather_kernel(
    groups, n, last, lhs, w_qkv, aux, full, auxs,
    own, parts, arrived, send_a, recv_a, send_b, recv_b, send_x, recv_x,
):
    g = lax.axis_index("groups")
    w = lax.axis_index("width")
    owners = groups * n
    me = g * n + w
    rows, size = full.shape[1:]
    barrier = pltpu.get_barrier_semaphore()

    @pl.loop(1, owners)
    def _(step):
        to = lax.rem(me + step, owners)
        pl.semaphore_signal(
            barrier, inc=1, device_id=at(to // n, lax.rem(to, n)), device_id_type=MESH
        )

    def piece(to):
        chunk = jnp.minimum(g * n + to, last)
        columns = pl.ds(pl.multiple_of(chunk * size, LANES), size)
        both = jnp.dot(lhs[...], w_qkv[:, columns], preferred_element_type=jnp.float32)
        return both[:rows] + both[rows:]

    @pl.loop(1, n)
    def _(step):
        parts[step] = piece(lax.rem(w + step, n)).astype(jnp.bfloat16)

    own[...] = piece(w)
    pl.semaphore_wait(barrier, owners - 1)

    def across(slot, shift):
        return pltpu.make_async_remote_copy(
            src_ref=aux, dst_ref=auxs.at[slot],
            send_sem=send_x.at[slot], recv_sem=recv_x.at[slot],
            device_id=at(g, lax.rem(w + shift + n, n)), device_id_type=MESH,
        )

    def scatter(step):
        return pltpu.make_async_remote_copy(
            src_ref=parts.at[step], dst_ref=arrived.at[step],
            send_sem=send_a.at[step], recv_sem=recv_a.at[step],
            device_id=at(g, lax.rem(w + step, n)), device_id_type=MESH,
        )

    @pl.loop(1, n)
    def _(step):
        scatter(step).start()

    moves = [across(0, -1), across(1, -2), across(2, 1)]
    for move in moves:
        move.start()

    @pl.loop(1, n)
    def _(step):
        scatter(step).wait_recv()

    def add(step, total):
        return total + arrived[step].astype(jnp.float32)

    full[me] = lax.fori_loop(1, n, add, own[...]).astype(jnp.bfloat16)

    def share(step):
        to = lax.rem(me + step, owners)
        return pltpu.make_async_remote_copy(
            src_ref=full.at[me], dst_ref=full.at[me],
            send_sem=send_b.at[step], recv_sem=recv_b.at[step],
            device_id=at(to // n, lax.rem(to, n)), device_id_type=MESH,
        )

    def shared(step):
        source = lax.rem(me - step + owners, owners)
        return pltpu.make_async_remote_copy(
            src_ref=full.at[source], dst_ref=full.at[source],
            send_sem=send_b.at[step], recv_sem=recv_b.at[step],
            device_id=at(source // n, lax.rem(source, n)), device_id_type=MESH,
        )

    @pl.loop(1, owners)
    def _(step):
        share(step).start()

    @pl.loop(1, owners)
    def _(step):
        shared(step).wait_recv()

    @pl.loop(1, n)
    def _(step):
        scatter(step).wait_send()

    @pl.loop(1, owners)
    def _(step):
        share(step).wait_send()

    for move in moves:
        move.wait()


def gather_folded(groups, n, lhs, w_qkv, aux):
    columns = w_qkv.shape[1]
    owners = groups * n
    third = columns // 3
    size = LANES * -(-columns // (LANES * owners))
    while third % size:
        size += LANES
    rows = lhs.shape[0] // 2
    dma = pltpu.SemaphoreType.DMA
    vmem = pl.BlockSpec(memory_space=pltpu.VMEM)
    return pl.pallas_call(
        functools.partial(gather_kernel, groups, n, columns // size - 1),
        name="gather_folded",
        out_shape=(
            jax.ShapeDtypeStruct((owners, rows, size), jnp.bfloat16),
            jax.ShapeDtypeStruct((3, *aux.shape), aux.dtype),
        ),
        in_specs=[vmem] * 3,
        out_specs=(vmem, vmem),
        scratch_shapes=[
            pltpu.VMEM((rows, size), jnp.float32),
            pltpu.VMEM((n, rows, size), jnp.bfloat16),
            pltpu.VMEM((n, rows, size), jnp.bfloat16),
            dma((n,)), dma((n,)), dma((owners,)), dma((owners,)), dma((3,)), dma((3,)),
        ],
        compiler_params=pltpu.CompilerParams(
            collective_id=0, has_side_effects=True, vmem_limit_bytes=32 << 20
        ),
    )(lhs, w_qkv, aux)


def column_map(shape, column_dim, parity, offset):
    column = lax.broadcasted_iota(jnp.int32, shape, column_dim)
    patch = lax.broadcasted_iota(jnp.int32, shape, 1 - column_dim)
    hit = column == 2 * patch + (parity + offset)
    return jnp.where(hit, 1.0, 0.0).astype(jnp.bfloat16)


def dot(a, b):
    return jnp.dot(a, b, preferred_element_type=jnp.float32)


def branch_kernel(
    offset_ref, own, auxs, mod, w_patch, full, w_out_hbm, w_final, out, pat, hid, rstd, att, w_out, sem
):
    load = pltpu.make_async_copy(w_out_hbm, w_out, sem)
    load.start()
    offset = offset_ref[0]
    area, columns = own.shape
    channels = w_patch.shape[0] // 4
    band = 2 * channels
    wide = jnp.concatenate([own[...], auxs[0, :area], auxs[1, :area]], axis=1).astype(jnp.bfloat16)
    spread = [dot(wide, column_map((3 * columns, columns), 0, b, offset)) for b in range(2)]
    for p in range(area // band):
        block = jnp.concatenate(
            [
                spread[b][p * band + a * channels : p * band + (a + 1) * channels]
                for a in range(2)
                for b in range(2)
            ],
            axis=0,
        )
        pat[p * columns : (p + 1) * columns] = block.T.astype(jnp.bfloat16)
    hid[...] = dot(pat[...], w_patch[...])
    hidden = hid[...]
    centered = hidden - jnp.mean(hidden, axis=1, keepdims=True)
    rstd[...] = jnp.broadcast_to(
        lax.rsqrt(jnp.mean(centered * centered, axis=1, keepdims=True) + epsilon), rstd.shape
    )
    features = w_patch.shape[0]
    size = full.shape[2]
    each = w_out.shape[0] // size
    row_head = lax.broadcasted_iota(jnp.int32, (size, size), 0) // HEAD
    col_head = lax.broadcasted_iota(jnp.int32, (size, size), 1) // HEAD
    same_head = jnp.where(row_head == col_head, 1.0 / HEAD, 0.0).astype(jnp.bfloat16)
    scale = math.log2(math.e) / math.sqrt(HEAD)
    ones = jnp.ones((pat.shape[0], HEAD), jnp.bfloat16)

    def project(i):
        block = full[i]
        return dot(pat[...], block[:features]) * rstd[:, :1] + block[features : features + 1].astype(
            jnp.float32
        )

    def head_norm(values):
        square = dot((values * values).astype(jnp.bfloat16), same_head)
        return values * lax.rsqrt(square + epsilon)

    @pl.loop(0, each)
    def _(j):
        queries = (head_norm(project(j)) * scale).astype(jnp.bfloat16)
        keys = head_norm(project(each + j)).astype(jnp.bfloat16)
        values = project(2 * each + j).astype(jnp.bfloat16)
        mixed = []
        for h in range(size // HEAD):
            cut = slice(h * HEAD, (h + 1) * HEAD)
            scores = lax.dot_general(
                queries[:, cut], keys[:, cut], (((1,), (1,)), ((), ())),
                preferred_element_type=jnp.float32,
            )
            weights = jnp.exp2(scores).astype(jnp.bfloat16)
            sums = dot(weights, jnp.concatenate([values[:, cut], ones], axis=1))
            mixed.append(sums[:, :HEAD] / sums[:, HEAD:])
        att[:, pl.ds(pl.multiple_of(j * size, LANES), size)] = jnp.concatenate(mixed, axis=1).astype(
            jnp.bfloat16
        )

    load.wait()
    step = 2 * columns
    for start in range(0, pat.shape[0], step):
        rows = slice(start, start + step)
        residual = hid[rows] + mod[2:3] * dot(att[rows], w_out[...])
        centered = residual - jnp.mean(residual, axis=1, keepdims=True)
        spread_of = jnp.mean(centered * centered, axis=1, keepdims=True)
        final_in = (centered * lax.rsqrt(spread_of + epsilon)).astype(jnp.bfloat16)
        tokens = dot(final_in, w_final[...])
        for i in range(step // columns):
            p = start // columns + i
            turned = tokens[i * columns : (i + 1) * columns].T.astype(jnp.bfloat16)
            laid = [dot(turned, column_map((columns, 3 * columns), 1, b, offset)) for b in range(2)]
            for a in range(2):
                low = a * band
                out[p * band + a * channels : p * band + (a + 1) * channels] = (
                    laid[0][low : low + channels] + laid[1][low + channels : low + band]
                ).astype(jnp.bfloat16)


def branch_velocity(offset, own, auxs, mod, w_patch, full, w_out, w_final):
    area, columns = own.shape
    tokens = area * 2 * columns // w_patch.shape[0]
    width = w_patch.shape[1]
    vmem = pl.BlockSpec(memory_space=pltpu.VMEM)
    return pl.pallas_call(
        branch_kernel,
        name="branch_velocity",
        out_shape=jax.ShapeDtypeStruct((area, 3 * columns), jnp.bfloat16),
        in_specs=[pl.BlockSpec(memory_space=pltpu.SMEM)]
        + [vmem] * 5
        + [pl.BlockSpec(memory_space=pl.ANY), vmem],
        out_specs=vmem,
        scratch_shapes=[
            pltpu.VMEM((tokens, w_patch.shape[0]), jnp.bfloat16),
            pltpu.VMEM((tokens, width), jnp.float32),
            pltpu.VMEM((tokens, LANES), jnp.float32),
            pltpu.VMEM((tokens, w_out.shape[0]), jnp.bfloat16),
            pltpu.VMEM(w_out.shape, w_out.dtype),
            pltpu.SemaphoreType.DMA,
        ],
        compiler_params=pltpu.CompilerParams(vmem_limit_bytes=56 << 20),
    )(offset, own, auxs, mod, w_patch, full, w_out, w_final)


def blend_kernel(
    n, sigma, v, own, counts, auxs, clean, border, other, outgoing, incoming, send_v, recv_v, send, recv
):
    g = lax.axis_index("groups")
    w = lax.axis_index("width")
    e = lax.axis_index("guide")
    area, columns = own.shape
    barrier = pltpu.get_barrier_semaphore()

    def place(shift):
        return at(g, lax.rem(w + shift + n, n))

    pl.semaphore_signal(barrier, inc=1, device_id={"guide": 1 - e}, device_id_type=MESH)
    for shift in (-2, -1, 1, 2):
        pl.semaphore_signal(barrier, inc=1, device_id=place(shift), device_id_type=MESH)
    pl.semaphore_wait(barrier, 5)
    swap = pltpu.make_async_remote_copy(
        src_ref=v, dst_ref=other, send_sem=send_v, recv_sem=recv_v,
        device_id={"guide": 1 - e}, device_id_type=MESH,
    )
    swap.start()
    swap.wait()
    mine = v[...].astype(jnp.float32)
    theirs = other[...].astype(jnp.float32)
    first = e == 0
    with_text = jnp.where(first, mine, theirs)
    plain = jnp.where(first, theirs, mine)
    guided = plain + guidance * (with_text - plain)
    here, ahead, further = (guided[:, i * columns : (i + 1) * columns] for i in range(3))
    lane = lax.broadcasted_iota(jnp.int32, (area, columns), 1)
    at_end = lane == columns - 1
    outgoing[0] = ahead.astype(jnp.bfloat16)
    outgoing[1] = jnp.where(at_end, here, further).astype(jnp.bfloat16)
    outgoing[2] = jnp.where(at_end, ahead, further).astype(jnp.bfloat16)
    outgoing[3] = here.astype(jnp.bfloat16)
    moves = [
        pltpu.make_async_remote_copy(
            src_ref=outgoing.at[i], dst_ref=incoming.at[i],
            send_sem=send.at[i], recv_sem=recv.at[i],
            device_id=place(shift), device_id_type=MESH,
        )
        for i, shift in enumerate((1, 1, 2, -1))
    ]
    for move in moves:
        move.start()
    for move in moves:
        move.wait()
    got = [incoming[i].astype(jnp.float32) for i in range(4)]
    total = here + got[0] + jnp.where(at_end, 0.0, got[2])
    clean[...] = own[...] - sigma[0] * (total / counts[:1])
    around = jnp.where(at_end, got[1] + got[2], got[3] + ahead + got[1])
    row_end = lax.broadcasted_iota(jnp.int32, (1, columns), 1) == columns - 1
    covered = jnp.where(row_end, auxs[2, area : area + 1], auxs[0, area : area + 1])
    latent = jnp.where(at_end, auxs[2, :area], auxs[0, :area])
    left = jnp.where(w > 0, 1.0, 0.0)
    right = jnp.where(w < n - 1, 1.0, 0.0)
    inside = jnp.where(at_end, left, right)
    border[...] = inside * (latent - sigma[0] * (around / covered))


def blend(n, sigma, v, own, counts, auxs):
    vmem = pl.BlockSpec(memory_space=pltpu.VMEM)
    dma = pltpu.SemaphoreType.DMA
    return pl.pallas_call(
        functools.partial(blend_kernel, n),
        name="blend",
        out_shape=(jax.ShapeDtypeStruct(own.shape, own.dtype),) * 2,
        in_specs=[pl.BlockSpec(memory_space=pltpu.SMEM)] + [vmem] * 4,
        out_specs=(vmem, vmem),
        scratch_shapes=[
            pltpu.VMEM(v.shape, v.dtype),
            pltpu.VMEM((4, *own.shape), jnp.bfloat16),
            pltpu.VMEM((4, *own.shape), jnp.bfloat16),
            dma, dma, dma((4,)), dma((4,)),
        ],
        compiler_params=pltpu.CompilerParams(
            collective_id=1, has_side_effects=True, vmem_limit_bytes=16 << 20
        ),
    )(sigma, v, own, counts, auxs)


def convolve(padded, w_dec):
    channels = padded.shape[0]
    height = padded.shape[1] - 2
    breadth = padded.shape[2] - 2
    shifted = [
        padded[:, row_at : row_at + height, col_at : col_at + breadth]
        for row_at in range(3)
        for col_at in range(3)
    ]
    stacked = jnp.stack(shifted).reshape(9 * channels, height * breadth)
    summed = lax.dot_general(
        stacked, w_dec, (((0,), (0,)), ((), ())), preferred_element_type=jnp.float32
    )
    return jax.nn.silu(summed).astype(jnp.bfloat16).reshape(height, breadth, w_dec.shape[1])


def shards(latent, starts, counts, step_index, cond_mod, w_patch, w_qkv, w_out, w_final, w_dec):
    groups, n = lax.axis_size("groups"), lax.axis_size("width")
    guide_at = lax.axis_index("guide")
    place = lax.axis_index("width")
    channels, height, columns = latent.shape
    half_rows = height // 2
    fraction = (step_index.astype(jnp.float32) + 1.0) / STEPS
    sigma = 3.0 * fraction / (1.0 + 2.0 * fraction)
    modulation = cond_mod[0]
    area = height * channels
    own = latent.transpose(1, 0, 2).reshape(area, columns)
    cover = jnp.broadcast_to(counts.astype(jnp.float32)[None], (8, columns))
    aux = jnp.concatenate([own, cover], axis=0)
    lhs = fold_rows(modulation, w_patch, w_qkv.shape[0], place)
    full, auxs = gather_folded(groups, n, lhs, w_qkv, aux)
    offset = starts - place * columns
    velocity = branch_velocity(offset, own, auxs, modulation, w_patch, full, w_out, w_final)
    clean, border = blend(n, sigma, velocity, own, cover, auxs)
    rows = clean.reshape(height, channels, columns)
    sides = border.reshape(height, channels, columns)
    denoised = lax.dynamic_slice_in_dim(rows, guide_at * half_rows, half_rows, 0).transpose(1, 0, 2)
    padded = jnp.concatenate([sides[:, :, -1:], rows, sides[:, :, :1]], axis=2).astype(jnp.bfloat16)
    padded = jnp.pad(padded, ((1, 1), (0, 0), (0, 0)))
    padded = lax.dynamic_slice_in_dim(padded, guide_at * half_rows, half_rows + 2, 0)
    features = convolve(padded.transpose(1, 0, 2), w_dec)
    return (denoised, features)


def solution(mesh):
    return jax.shard_map(
        shards,
        mesh=mesh,
        in_specs=(
            P(None, None, ("groups", "width")),
            P(("groups", "width")),
            P(("groups", "width")),
            P("groups"),
            P("guide", None, None),
            P(),
            P("width", None),
            P(),
            P(),
            P(),
        ),
        out_specs=(P(None, "guide", ("groups", "width")), P("guide", ("groups", "width"), None)),
        check_vma=False,
    )
```

time: 285 us -> 78.9 us (0.28)
  waiting for transfers between devices: 146 us -> 0 us
  Pallas kernels: 0 us -> 60.6 us
  matrix products: 55.3 us -> 1.29 us
  starting transfers between devices: 18.3 us -> 0 us
  local copies, waits for them, and re-layouts: 28.5 us -> 10.6 us
  between operations: 15.8 us -> 2.2 us
  other arithmetic: 16.8 us -> 3.76 us
  blocking collectives: 3.79 us -> 0 us
    all_gather x1 -> x0, waiting for transfers between devices: 115 us -> none  [shards(): lax.all_gather(weight_half, 'width', axis=0, tiled=True)]
    pallas_call x0 -> x3, Pallas kernels: none -> 60.6 us  [the longest x1 30.5 us: gather_folded(): pl.pallas_call(functools.partial(gather_kernel, groups, n, columns // siz...]
    dot_general x5 -> x0, matrix products: 41 us -> none  [the longest x1 23 us: shards(): jnp.dot(both_rows, lax.all_gather(weight_half, 'width', axis=0, tiled=Tru...]
    ppermute x9 -> x0, waiting for transfers between devices: 19.4 us -> none  [the longest x4 13.3 us: from_behind(): return lax.ppermute(x, axis, [(i, (i + by) % peers) for i in range(peers)])]
    ppermute x9 -> x0, starting transfers between devices: 18.2 us -> none  [the longest x4 13.1 us: from_behind(): return lax.ppermute(x, axis, [(i, (i + by) % peers) for i in range(peers)])]
    dot_general x1 -> x0, local copies, waits for them, and re-layouts: 13.3 us -> none  [shards(): jnp.dot(both_rows, lax.all_gather(weight_half, 'width', axis=0, tiled=Tru...]
    sub x1 -> x0, matrix products: 13 us -> none  [attend(): weights = jax.nn.softmax(scores, axis=-1).astype(jnp.bfloat16)]
    reduce_scatter x1 -> x0, waiting for transfers between devices: 11.1 us -> none  [shards(): lax.psum_scatter(partial_value.astype(jnp.bfloat16), 'guide', scatter_dim...]
  transfers between devices with their start and end apart: 11 -> 0, of which waited for: 9 -> 0; matrix products, arithmetic and copies ran while one was open for 8% -> 0% of each run, Pallas kernels for 0% -> 0%
where the time goes in v2:
time: 78.9 us; the launch traced here: 78.4 us
  Pallas kernels  60.6 us (77%)
  local copies, waits for them, and re-layouts  10.6 us (13%)
  other arithmetic  3.76 us (5%)
  between operations  2.2 us (3%)
  matrix products  1.29 us (2%)
    pallas_call x1, Pallas kernels, gather_folded(): pl.pallas_call(functools.partial(gather_kernel, groups, n, columns // siz...  30.5 us
    pallas_call x1, Pallas kernels, branch_velocity(): pl.pallas_call(branch_kernel, name='branch_velocity', out_shape=jax.Shape...  20.2 us
    pallas_call x1, Pallas kernels, blend(): pl.pallas_call(functools.partial(blend_kernel, n), name='blend', out_shap...  9.93 us
    unnamed x28, local copies, waits for them, and re-layouts  8.86 us

profile of v2, /device:TPU:0, one launch (start us, length us, event | category | flops | bytes accessed | tf_op | source)
XLA Modules:
  0.0 78.4 jit_solution(13147808079515902978)
XLA Ops:
  0.6 0.0 copy-start
  0.7 0.8 %fusion.14 = (f32[304]{0:T(512)S(1)}, f32[1,304]{1,0:T(1,128)S(1)}) fusion(f32[1,3,2432]{2,0,1:T(1,128)} %param.14, s32[]{:T(128)S(6)} %add.47, s32[]{:T(128)S(6)} %select_n.10), kind=kLoop, calls=%fused_computation.49 | loop fusion | flops 304 | bytes 4872 | tf_op jit(solution)/shard_map/add | solution.py:30
  1.5 1.1 %convert_reduce_fusion = f32[64]{0:T(128)S(1)} fusion(bf16[64,2432]{1,0:T(8,128)(2,1)} %w_patch.1), kind=kLoop, calls=%fused_computation.1 | loop fusion | flops 311232 | bytes 311552 | tf_op jit(solution)/shard_map/reduce_sum | solution.py:27
  2.6 0.9 %subtract_multiply_fusion = f32[64,304]{1,0:T(8,128)S(1)} fusion(f32[304]{0:T(512)S(1)} %get-tuple-element.14, f32[64]{0:T(128)S(1)} %broadcast_multiply_fusion, bf16[64,2432]{1,0:T(8,128)(2,1)} %w_patch.1, s32[]{:T(128)S(6)} %select_n.10), kind=kLoop, calls=%fused_computation.17 | loop fusion | flops 58368 | bytes 118212 | tf_op jit(solution)/shard_map/mul | solution.py:30
  3.6 0.9 %copy.15 = f32[8,16,128]{2,1,0:T(8,128)S(1)} copy(f32[8,16,128]{2,0,1:T(8,128)} %bitcast.64) | data formatting | bytes 131072 | tf_op jit(solution)/shard_map/transpose | solution.py:397
  4.5 0.0 copy-start.2
  4.5 0.7 convert_element_type.31
  5.2 0.0 copy-start.1
  5.2 1.7 %copy-done.1 = bf16[304,3840]{1,0:T(8,128)(2,1)S(1)} copy-done((bf16[304,3840]{1,0:T(8,128)(2,1)S(1)}, bf16[304,3840]{1,0:T(8,128)(2,1)}, u32[]{:S(2)}) %copy-start.1) | copy-done | bytes 2334744
  6.8 30.5 %gather_folded.1 = (bf16[16,80,256]{2,1,0:T(8,128)(2,1)S(1)}, f32[3,136,128]{2,1,0:T(8,128)S(1)}) custom-call(bf16[160,304]{1,0:T(8,128)(2,1)S(1)} %pad_maximum_fusion.lhs, bf16[304,3840]{1,0:T(8,128)(2,1)S(1)} %copy-done.1, f32[136,128]{1,0:T(8,128)S(1)} %pad_maximum_fusion.1.aux), custom_call_target="tpu_custom_call" | custom-call | tf_op jit(solution)/shard_map/gather_folded/pallas_call | solution.py:148
  37.3 0.0 copy-start.4
  37.3 0.7 copy-done.4
  38.0 0.0 copy-start.6
  38.0 0.8 %copy-done.6 = bf16[16,80,256]{2,1,0:T(8,128)(2,1)} copy-done((bf16[16,80,256]{2,1,0:T(8,128)(2,1)}, bf16[16,80,256]{2,1,0:T(8,128)(2,1)S(1)}, u32[]{:S(2)}) %copy-start.6) | copy-done | bytes 655384
  38.8 0.0 copy-start.5
  39.5 2.0 %copy.16.w_final = bf16[2432,64]{1,0:T(8,128)(2,1)} copy(bf16[2432,64]{0,1:T(8,128)(2,1)} %param.18) | data formatting | bytes 622592 | tf_op args[8]
  41.6 1.4 %copy.32 = f32[1,3,2432]{2,1,0:T(4,128)} copy(f32[1,3,2432]{2,0,1:T(1,128)} %param.14) | data formatting | bytes 58368
  42.9 0.0 copy-done.2
  42.9 20.2 %branch_velocity.1.v = bf16[128,384]{1,0:T(8,128)(2,1)} custom-call(s32[1]{0:T(128)S(6)} %sub.18.offset_ref, f32[128,128]{1,0:T(8,128)} %bitcast.58, f32[3,136,128]{2,1,0:T(8,128)} %copy-done.4, f32[3,2432]{1,0:T(4,128)} %bitcast.63, bf16[64,2432]{1,0:T(8,128)(2,1)} %w_patch.1, bf16[16,80,256]{2,1,0:T(8,128)(2,1)} %copy-done.6, ...), custom_call_target="tpu_custom_call" | custom-call | tf_op jit(solution)/shard_map/branch_velocity/pallas_call | solution.py:270
  63.8 0.0 copy-done.5
  63.9 0.0 copy-start.3
  63.9 0.8 %copy-done.3 = f32[8,16,128]{2,1,0:T(8,128)S(1)} copy-done((f32[8,16,128]{2,1,0:T(8,128)S(1)}, f32[8,16,128]{2,1,0:T(8,128)}, u32[]{:S(2)}) %copy-start.3) | copy-done | bytes 65560
  64.7 0.0 copy-start.7
  64.7 0.9 %copy-done.7 = bf16[128,384]{1,0:T(8,128)(2,1)S(1)} copy-done((bf16[128,384]{1,0:T(8,128)(2,1)S(1)}, bf16[128,384]{1,0:T(8,128)(2,1)}, u32[]{:S(2)}) %copy-start.7) | copy-done | bytes 98328
  65.6 9.9 %blend.1 = (f32[128,128]{1,0:T(8,128)S(1)}, f32[128,128]{1,0:T(8,128)S(1)}) custom-call(f32[1]{0:T(128)S(6)} %div.14.sigma, bf16[128,384]{1,0:T(8,128)(2,1)S(1)} %copy-done.7, f32[128,128]{1,0:T(8,128)S(1)} %bitcast.59, f32[8,128]{1,0:T(8,128)S(1)} %broadcast_in_dim.2.counts, f32[3,136,128]{2,1,0:T(8,128)S(1)} %copy-done.5), custom_call_target="tpu_custom_call" | custom-call | tf_op jit(solution)/shard_map/blend/pallas_call | solution.py:353
  75.5 0.1 fusion.15
  75.7 0.1 fusion.9
  75.8 0.1 constant_dynamic-update-slice_fusion.7
  75.9 0.1 constant_dynamic-update-slice_fusion.6
  76.1 0.1 constant_dynamic-update-slice_fusion.4
  76.2 0.1 constant_dynamic-update-slice_fusion.3
  76.3 0.1 constant_dynamic-update-slice_fusion.1
  76.4 0.1 constant_dynamic-update-slice_fusion
  76.5 0.0 copy-done
  76.5 1.3 %multiply_convert_fusion = bf16[512,512]{1,0:T(8,128)(2,1)} fusion(bf16[144,512]{1,0:T(8,128)(2,1)S(1)} %copy-done, bf16[18,8,4,128]{3,2,1,0:T(4,128)(2,1)S(1)} %bitcast.65), kind=kOutput, calls=%fused_computation | convolution fusion | flops 76808192 | bytes 819200 | tf_op jit(solution)/shard_map/dot_general | solution.py:381
  77.8 0.6 dynamic-slice_bitcast_fusion
  (13 shorter events, 0.2 us)
Async XLA Ops:
  0.6 75.9 %copy-start = (bf16[144,512]{1,0:T(8,128)(2,1)S(1)}, bf16[144,512]{1,0:T(8,128)(2,1)}, u32[]{:S(2)}) copy-start(bf16[144,512]{1,0:T(8,128)(2,1)} %param.19) | copy-start | bytes 442372
  4.5 38.5 %copy-start.2 = (f32[8,16,128]{2,1,0:T(8,128)}, f32[8,16,128]{2,1,0:T(8,128)S(1)}, u32[]{:S(2)}) copy-start(f32[8,16,128]{2,1,0:T(8,128)S(1)} %copy.15) | copy-start | bytes 196612
  5.2 1.7 %copy-start.1 = (bf16[304,3840]{1,0:T(8,128)(2,1)S(1)}, bf16[304,3840]{1,0:T(8,128)(2,1)}, u32[]{:S(2)}) copy-start(bf16[304,3840]{1,0:T(8,128)(2,1)} %w_qkv.1) | copy-start | bytes 7004164
  37.3 0.7 copy-start.4
  38.0 0.8 %copy-start.6 = (bf16[16,80,256]{2,1,0:T(8,128)(2,1)}, bf16[16,80,256]{2,1,0:T(8,128)(2,1)S(1)}, u32[]{:S(2)}) copy-start(bf16[16,80,256]{2,1,0:T(8,128)(2,1)S(1)} %get-tuple-element.7.full) | copy-start | bytes 1966084
  38.8 25.0 %copy-start.5 = (f32[3,136,128]{2,1,0:T(8,128)S(1)}, f32[3,136,128]{2,1,0:T(8,128)}, u32[]{:S(2)}) copy-start(f32[3,136,128]{2,1,0:T(8,128)} %copy-done.4) | copy-start | bytes 626692
  63.9 0.8 %copy-start.3 = (f32[8,16,128]{2,1,0:T(8,128)S(1)}, f32[8,16,128]{2,1,0:T(8,128)}, u32[]{:S(2)}) copy-start(f32[8,16,128]{2,1,0:T(8,128)} %copy-done.2) | copy-start | bytes 196612
  64.7 0.9 %copy-start.7 = (bf16[128,384]{1,0:T(8,128)(2,1)S(1)}, bf16[128,384]{1,0:T(8,128)(2,1)}, u32[]{:S(2)}) copy-start(bf16[128,384]{1,0:T(8,128)(2,1)} %branch_velocity.1.v) | copy-start | bytes 294916

commit v3 on v0

v3 whole, which is shorter than its diff:
```python
import functools
import math

import jax
import jax.numpy as jnp
from jax import lax
from jax.experimental import pallas as pl
from jax.experimental.pallas import tpu as pltpu
from jax.sharding import PartitionSpec as P

HEAD = 64
STEPS = 28
LANES = 128
MESH = pl.DeviceIdType.MESH

guidance = 4.0
epsilon = 1e-06


def at(groups, width):
    return {"groups": groups, "width": width}


def column_map(shape, column_dim, parity, offset):
    column = lax.broadcasted_iota(jnp.int32, shape, column_dim)
    patch = lax.broadcasted_iota(jnp.int32, shape, 1 - column_dim)
    hit = column == 2 * patch + (parity + offset)
    return jnp.where(hit, 1.0, 0.0).astype(jnp.bfloat16)


def dot(a, b):
    return jnp.dot(a, b, preferred_element_type=jnp.float32)


def row_map(shape, natural_dim, channels, height):
    natural = lax.broadcasted_iota(jnp.int32, shape, natural_dim)
    moved = lax.broadcasted_iota(jnp.int32, shape, 1 - natural_dim)
    hit = natural == lax.rem(moved, channels) * height + moved // channels
    return jnp.where(hit, 1.0, 0.0).astype(jnp.bfloat16)


def fold_rows(modulation, w_patch, depth, w):
    patch = w_patch[...].astype(jnp.float32)
    patch = patch - jnp.mean(patch, axis=1, keepdims=True)
    shift = jnp.broadcast_to(modulation[0:1], (16, patch.shape[1]))
    rows = jnp.concatenate([patch * (1.0 + modulation[1:2]), shift], axis=0)
    total = rows.shape[1]
    rows = pltpu.roll(rows, lax.rem(total - w * depth, total), 1)[:, :depth]
    high = rows.astype(jnp.bfloat16)
    return high, (rows - high.astype(jnp.float32)).astype(jnp.bfloat16)


def step_kernel(
    groups, n,
    offset_ref, sigma, latent, counts, mod, w_patch, w_final, w_qkv_hbm, w_out_hbm,
    clean, border,
    w_qkv, w_out, high, low, soft, edges, softs, edge_pair, parts, arrived, full, shifts,
    pat, rstd, att, turned_v, v, other, outgoing, incoming,
    load_sem, send_a, recv_a, send_b, recv_b, send_x, recv_x, send_v, recv_v, send, recv,
):
    g = lax.axis_index("groups")
    w = lax.axis_index("width")
    e = lax.axis_index("guide")
    owners = groups * n
    me = g * n + w
    features, size = full.shape[1:]
    area, columns = latent.shape
    channels = features // 4
    height = area // channels
    band = 2 * channels
    pieces = w_qkv.shape[1] // size
    barrier = pltpu.get_barrier_semaphore()

    @pl.loop(1, owners)
    def _(step):
        to = lax.rem(me + step, owners)
        pl.semaphore_signal(
            barrier, inc=1, device_id=at(to // n, lax.rem(to, n)), device_id_type=MESH
        )

    pl.semaphore_signal(barrier, inc=1, device_id={"guide": 1 - e}, device_id_type=MESH)
    load_qkv = pltpu.make_async_copy(w_qkv_hbm, w_qkv, load_sem.at[0])
    load_out = pltpu.make_async_copy(w_out_hbm, w_out, load_sem.at[1])
    load_qkv.start()
    load_out.start()

    own = latent[...]
    soft[...] = own.astype(jnp.bfloat16)
    turned = own.T
    cover = counts[...].astype(jnp.float32)
    edges[...] = jnp.concatenate(
        [turned[:1], turned[columns - 1 :], cover, jnp.zeros((5, columns), jnp.float32)], axis=0
    )
    high_rows, low_rows = fold_rows(mod, w_patch, w_qkv.shape[0], w)
    high[...] = high_rows
    low[...] = low_rows
    load_qkv.wait()

    @pl.loop(0, n)
    def _(step):
        chunk = jnp.minimum(g * n + lax.rem(w + step, n), pieces - 1)
        cut = w_qkv[:, pl.ds(pl.multiple_of(chunk * size, LANES), size)]
        parts[step] = (dot(high[:features], cut) + dot(low[:features], cut)).astype(jnp.bfloat16)

    @pl.when(g == pieces // n)
    def _():
        line = dot(high[features:], w_qkv[...]) + dot(low[features:], w_qkv[...])
        lines = jnp.concatenate([line[:1, i * size : (i + 1) * size] for i in range(pieces)], axis=0)
        lines = jnp.concatenate(
            [lines, jnp.zeros((features - pieces, size), jnp.float32)], axis=0
        )
        parts[lax.rem(pieces % n - w + n, n)] = lines.astype(jnp.bfloat16)

    pl.semaphore_wait(barrier, owners)

    def remote(source, target, sent, received, shift):
        return pltpu.make_async_remote_copy(
            src_ref=source, dst_ref=target, send_sem=sent, recv_sem=received,
            device_id=at(g, lax.rem(w + shift + n, n)), device_id_type=MESH,
        )

    def scatter(step):
        return remote(parts.at[step], arrived.at[step], send_a.at[step], recv_a.at[step], step)

    @pl.loop(1, n)
    def _(step):
        scatter(step).start()

    moves = [
        remote(soft, softs.at[0], send_x.at[0], recv_x.at[0], -1),
        remote(soft, softs.at[1], send_x.at[1], recv_x.at[1], -2),
        remote(edges, edge_pair.at[0], send_x.at[2], recv_x.at[2], -1),
        remote(edges, edge_pair.at[1], send_x.at[3], recv_x.at[3], 1),
    ]
    for move in moves:
        move.start()

    @pl.loop(1, n)
    def _(step):
        scatter(step).wait_recv()

    def add(step, total):
        return total + arrived[step].astype(jnp.float32)

    full[me] = lax.fori_loop(1, n, add, parts[0].astype(jnp.float32)).astype(jnp.bfloat16)

    def shared(step, peer, source):
        return pltpu.make_async_remote_copy(
            src_ref=full.at[source], dst_ref=full.at[source],
            send_sem=send_b.at[step], recv_sem=recv_b.at[step],
            device_id=at(peer // n, lax.rem(peer, n)), device_id_type=MESH,
        )

    @pl.loop(1, owners)
    def _(step):
        shared(step, lax.rem(me + step, owners), me).start()

    for move in moves:
        move.wait()
    offset = offset_ref[0]
    wide = jnp.concatenate([soft[...], softs[0], softs[1]], axis=1)
    wide = dot(row_map((area, area), 1, channels, height), wide).astype(jnp.bfloat16)
    spread = [dot(wide, column_map((3 * columns, columns), 0, b, offset)) for b in range(2)]
    for p in range(area // band):
        block = jnp.concatenate(
            [
                spread[b][p * band + a * channels : p * band + (a + 1) * channels]
                for a in range(2)
                for b in range(2)
            ],
            axis=0,
        )
        pat[p * columns : (p + 1) * columns] = block.T.astype(jnp.bfloat16)
    tokens = pat.shape[0]
    step_rows = 2 * columns
    for start in range(0, tokens, step_rows):
        rows = slice(start, start + step_rows)
        hidden = dot(pat[rows], w_patch[...])
        centered = hidden - jnp.mean(hidden, axis=1, keepdims=True)
        rstd[rows] = jnp.broadcast_to(
            lax.rsqrt(jnp.mean(centered * centered, axis=1, keepdims=True) + epsilon),
            (step_rows, rstd.shape[1]),
        )
    each = w_out.shape[0] // size
    row_head = lax.broadcasted_iota(jnp.int32, (size, size), 0) // HEAD
    col_head = lax.broadcasted_iota(jnp.int32, (size, size), 1) // HEAD
    same_head = jnp.where(row_head == col_head, 1.0 / HEAD, 0.0).astype(jnp.bfloat16)
    scale = math.log2(math.e) / math.sqrt(HEAD)
    ones = jnp.ones((tokens, HEAD), jnp.bfloat16)

    @pl.loop(1, owners)
    def _(step):
        source = lax.rem(me - step + owners, owners)
        shared(step, source, source).wait_recv()

    shifts[...] = full[pieces].astype(jnp.float32)

    def project(i):
        return dot(pat[...], full[i]) * rstd[:, :1] + shifts[pl.ds(i, 1)]

    def head_norm(values):
        square = dot((values * values).astype(jnp.bfloat16), same_head)
        return values * lax.rsqrt(square + epsilon)

    @pl.loop(0, each)
    def _(j):
        queries = (head_norm(project(j)) * scale).astype(jnp.bfloat16)
        keys = head_norm(project(each + j)).astype(jnp.bfloat16)
        values = project(2 * each + j).astype(jnp.bfloat16)
        mixed = []
        for h in range(size // HEAD):
            cut = slice(h * HEAD, (h + 1) * HEAD)
            scores = lax.dot_general(
                queries[:, cut], keys[:, cut], (((1,), (1,)), ((), ())),
                preferred_element_type=jnp.float32,
            )
            weights = jnp.exp2(scores).astype(jnp.bfloat16)
            sums = dot(weights, jnp.concatenate([values[:, cut], ones], axis=1))
            mixed.append(sums[:, :HEAD] / sums[:, HEAD:])
        att[:, pl.ds(pl.multiple_of(j * size, LANES), size)] = jnp.concatenate(mixed, axis=1).astype(
            jnp.bfloat16
        )

    load_out.wait()
    for start in range(0, tokens, step_rows):
        rows = slice(start, start + step_rows)
        residual = dot(pat[rows], w_patch[...]) + mod[2:3] * dot(att[rows], w_out[...])
        centered = residual - jnp.mean(residual, axis=1, keepdims=True)
        spread_of = jnp.mean(centered * centered, axis=1, keepdims=True)
        final_in = (centered * lax.rsqrt(spread_of + epsilon)).astype(jnp.bfloat16)
        found = lax.dot_general(
            final_in, w_final[...], (((1,), (1,)), ((), ())), preferred_element_type=jnp.float32
        )
        for i in range(step_rows // columns):
            p = start // columns + i
            turned = found[i * columns : (i + 1) * columns].T.astype(jnp.bfloat16)
            laid = [dot(turned, column_map((columns, 3 * columns), 1, b, offset)) for b in range(2)]
            for a in range(2):
                at_row = a * band
                turned_v[p * band + a * channels : p * band + (a + 1) * channels] = (
                    laid[0][at_row : at_row + channels] + laid[1][at_row + channels : at_row + band]
                ).astype(jnp.bfloat16)
    v[...] = dot(row_map((area, area), 0, channels, height), turned_v[...]).astype(jnp.bfloat16)

    swap = pltpu.make_async_remote_copy(
        src_ref=v, dst_ref=other, send_sem=send_v, recv_sem=recv_v,
        device_id={"guide": 1 - e}, device_id_type=MESH,
    )
    swap.start()
    swap.wait()
    mine = v[...].astype(jnp.float32)
    theirs = other[...].astype(jnp.float32)
    first = e == 0
    with_text = jnp.where(first, mine, theirs)
    plain = jnp.where(first, theirs, mine)
    guided = plain + guidance * (with_text - plain)
    here, ahead, further = (guided[:, i * columns : (i + 1) * columns] for i in range(3))
    at_end = lax.broadcasted_iota(jnp.int32, (area, columns), 1) == columns - 1
    outgoing[0] = ahead.astype(jnp.bfloat16)
    outgoing[1] = jnp.where(at_end, here, further).astype(jnp.bfloat16)
    outgoing[2] = jnp.where(at_end, ahead, further).astype(jnp.bfloat16)
    outgoing[3] = here.astype(jnp.bfloat16)
    moves = [
        remote(outgoing.at[i], incoming.at[i], send.at[i], recv.at[i], shift)
        for i, shift in enumerate((1, 1, 2, -1))
    ]
    for move in moves:
        move.start()

    @pl.loop(1, n)
    def _(step):
        scatter(step).wait_send()

    @pl.loop(1, owners)
    def _(step):
        shared(step, lax.rem(me + step, owners), me).wait_send()

    for move in moves:
        move.wait()
    got = [incoming[i].astype(jnp.float32) for i in range(4)]
    total = here + got[0] + jnp.where(at_end, 0.0, got[2])
    clean[...] = own - sigma[0] * (total / cover)
    around = jnp.where(at_end, got[1] + got[2], got[3] + ahead + got[1])
    row_end = lax.broadcasted_iota(jnp.int32, (1, columns), 1) == columns - 1
    right_edges, left_edges = edge_pair[0], edge_pair[1]
    covered = jnp.where(row_end, left_edges[2:3], right_edges[2:3])
    beside = jnp.where(at_end, left_edges.T[:, 1:2], right_edges.T[:, 0:1])
    left = jnp.where(w > 0, 1.0, 0.0)
    right = jnp.where(w < n - 1, 1.0, 0.0)
    border[...] = jnp.where(at_end, left, right) * (beside - sigma[0] * (around / covered))


def run_step(groups, n, offset, sigma, own, counts, mod, w_patch, w_final, w_qkv, w_out):
    total = w_qkv.shape[1]
    owners = groups * n
    size = LANES * -(-total // (LANES * owners))
    while (total // 3) % size or total // size >= owners:
        size += LANES
    area, columns = own.shape
    features = w_patch.shape[0]
    tokens = area * 2 * columns // features
    dma = pltpu.SemaphoreType.DMA
    vmem = pl.BlockSpec(memory_space=pltpu.VMEM)
    smem = pl.BlockSpec(memory_space=pltpu.SMEM)
    hbm = pl.BlockSpec(memory_space=pl.ANY)
    half, single = jnp.bfloat16, jnp.float32
    return pl.pallas_call(
        functools.partial(step_kernel, groups, n),
        name="guided_step",
        out_shape=(jax.ShapeDtypeStruct(own.shape, own.dtype),) * 2,
        in_specs=[smem] * 2 + [vmem] * 5 + [hbm] * 2,
        out_specs=(vmem, vmem),
        scratch_shapes=[
            pltpu.VMEM(w_qkv.shape, half),
            pltpu.VMEM(w_out.shape, half),
            pltpu.VMEM((features + 16, w_qkv.shape[0]), half),
            pltpu.VMEM((features + 16, w_qkv.shape[0]), half),
            pltpu.VMEM(own.shape, half),
            pltpu.VMEM((8, columns), single),
            pltpu.VMEM((2, *own.shape), half),
            pltpu.VMEM((2, 8, columns), single),
            pltpu.VMEM((n, features, size), half),
            pltpu.VMEM((n, features, size), half),
            pltpu.VMEM((owners, features, size), half),
            pltpu.VMEM((features, size), single),
            pltpu.VMEM((tokens, features), half),
            pltpu.VMEM((tokens, LANES), single),
            pltpu.VMEM((tokens, w_out.shape[0]), half),
            pltpu.VMEM((area, 3 * columns), half),
            pltpu.VMEM((area, 3 * columns), half),
            pltpu.VMEM((area, 3 * columns), half),
            pltpu.VMEM((4, *own.shape), half),
            pltpu.VMEM((4, *own.shape), half),
            dma((2,)), dma((n,)), dma((n,)), dma((owners,)), dma((owners,)), dma((4,)), dma((4,)),
            dma, dma, dma((4,)), dma((4,)),
        ],
        compiler_params=pltpu.CompilerParams(
            collective_id=0, has_side_effects=True, vmem_limit_bytes=56 << 20
        ),
    )(offset, sigma, own, counts, mod, w_patch, w_final, w_qkv, w_out)


def convolve(padded, w_dec):
    channels = padded.shape[0]
    height = padded.shape[1] - 2
    breadth = padded.shape[2] - 2
    shifted = [
        padded[:, row_at : row_at + height, col_at : col_at + breadth]
        for row_at in range(3)
        for col_at in range(3)
    ]
    stacked = jnp.stack(shifted).reshape(9 * channels, height * breadth)
    summed = lax.dot_general(
        stacked, w_dec, (((0,), (0,)), ((), ())), preferred_element_type=jnp.float32
    )
    return jax.nn.silu(summed).astype(jnp.bfloat16).reshape(height, breadth, w_dec.shape[1])


def shards(latent, starts, counts, step_index, cond_mod, w_patch, w_qkv, w_out, w_final, w_dec):
    groups, n = lax.axis_size("groups"), lax.axis_size("width")
    guide_at = lax.axis_index("guide")
    place = lax.axis_index("width")
    channels, height, columns = latent.shape
    half_rows = height // 2
    fraction = (step_index.astype(jnp.float32) + 1.0) / STEPS
    sigma = 3.0 * fraction / (1.0 + 2.0 * fraction)
    own = latent.reshape(channels * height, columns)
    offset = starts - place * columns
    clean, border = run_step(
        groups, n, offset, sigma, own, counts[None], cond_mod[0], w_patch, w_final.T, w_qkv, w_out
    )
    rows = clean.reshape(latent.shape)
    sides = border.reshape(latent.shape)
    denoised = lax.dynamic_slice_in_dim(rows, guide_at * half_rows, half_rows, 1)
    padded = jnp.concatenate([sides[:, :, -1:], rows, sides[:, :, :1]], axis=2).astype(jnp.bfloat16)
    padded = jnp.pad(padded, ((0, 0), (1, 1), (0, 0)))
    padded = lax.dynamic_slice_in_dim(padded, guide_at * half_rows, half_rows + 2, 1)
    features = convolve(padded, w_dec)
    return (denoised, features)


def solution(mesh):
    return jax.shard_map(
        shards,
        mesh=mesh,
        in_specs=(
            P(None, None, ("groups", "width")),
            P(("groups", "width")),
            P(("groups", "width")),
            P("groups"),
            P("guide", None, None),
            P(),
            P("width", None),
            P(),
            P(),
            P(),
        ),
        out_specs=(P(None, "guide", ("groups", "width")), P("guide", ("groups", "width"), None)),
        check_vma=False,
    )
```

time: 285 us -> 63 us (0.22)
  waiting for transfers between devices: 146 us -> 0 us
  Pallas kernels: 0 us -> 54.8 us
  matrix products: 55.3 us -> 1.29 us
  local copies, waits for them, and re-layouts: 28.5 us -> 3.57 us
  starting transfers between devices: 18.3 us -> 0 us
  other arithmetic: 16.8 us -> 1.01 us
  between operations: 15.8 us -> 2.06 us
  blocking collectives: 3.79 us -> 0 us
    all_gather x1 -> x0, waiting for transfers between devices: 115 us -> none  [shards(): lax.all_gather(weight_half, 'width', axis=0, tiled=True)]
    pallas_call x0 -> x1, Pallas kernels: none -> 54.8 us  [run_step(): pl.pallas_call(functools.partial(step_kernel, groups, n), name='guided_st...]
    dot_general x5 -> x0, matrix products: 41 us -> none  [the longest x1 23 us: shards(): jnp.dot(both_rows, lax.all_gather(weight_half, 'width', axis=0, tiled=Tru...]
    ppermute x9 -> x0, waiting for transfers between devices: 19.4 us -> none  [the longest x4 13.3 us: from_behind(): return lax.ppermute(x, axis, [(i, (i + by) % peers) for i in range(peers)])]
    ppermute x9 -> x0, starting transfers between devices: 18.2 us -> none  [the longest x4 13.1 us: from_behind(): return lax.ppermute(x, axis, [(i, (i + by) % peers) for i in range(peers)])]
    dot_general x1 -> x0, local copies, waits for them, and re-layouts: 13.3 us -> none  [shards(): jnp.dot(both_rows, lax.all_gather(weight_half, 'width', axis=0, tiled=Tru...]
    sub x1 -> x0, matrix products: 13 us -> none  [attend(): weights = jax.nn.softmax(scores, axis=-1).astype(jnp.bfloat16)]
    reduce_scatter x1 -> x0, waiting for transfers between devices: 11.1 us -> none  [shards(): lax.psum_scatter(partial_value.astype(jnp.bfloat16), 'guide', scatter_dim...]
  transfers between devices with their start and end apart: 11 -> 0, of which waited for: 9 -> 0; matrix products, arithmetic and copies ran while one was open for 8% -> 0% of each run, Pallas kernels for 0% -> 0%
where the time goes in v3:
time: 63 us; the launch traced here: 62.7 us
  Pallas kernels  54.8 us (87%)
  local copies, waits for them, and re-layouts  3.57 us (6%)
  between operations  2.06 us (3%)
  matrix products  1.29 us (2%)
  other arithmetic  1.01 us (2%)
    pallas_call x1, Pallas kernels, run_step(): pl.pallas_call(functools.partial(step_kernel, groups, n), name='guided_st...  54.8 us
    unnamed x11, local copies, waits for them, and re-layouts  1.92 us
    dynamic_slice x1, local copies, waits for them, and re-layouts, shards(): lax.dynamic_slice_in_dim(rows, guide_at * half_rows, half_rows, 1)  1.47 us
    dot_general x1, matrix products, convolve(): lax.dot_general(stacked, w_dec, (((0,), (0,)), ((), ())), preferred_eleme...  1.29 us

profile of v3, /device:TPU:0, one launch (start us, length us, event | category | flops | bytes accessed | tf_op | source)
XLA Modules:
  0.0 62.7 jit_solution(1010302367040341768)
XLA Ops:
  0.6 0.0 copy-start
  2.0 1.4 %copy.19 = f32[1,3,2432]{2,1,0:T(4,128)} copy(f32[1,3,2432]{2,0,1:T(1,128)} %param.14) | data formatting | bytes 58368
  3.4 54.8 %guided_step.1 = (f32[128,128]{1,0:T(8,128)}, f32[128,128]{1,0:T(8,128)}) custom-call(s32[1]{0:T(128)S(6)} %sub.7.offset_ref, f32[1]{0:T(128)S(6)} %div.8.sigma, f32[128,128]{1,0:T(8,128)} %bitcast.57, s32[1,128]{1,0:T(1,128)} %bitcast.59, f32[3,2432]{1,0:T(4,128)} %bitcast.55, bf16[64,2432]{1,0:T(8,128)(2,1)} %w_patch.1, bf16[64,2432]{1,0:T(8,128)(2,1)} %bitcast.54, ...), custom_call_target="tpu_custom_call" | custom-call | tf_op jit(solution)/shard_map/guided_step/pallas_call | solution.py:307
  58.2 0.9 %convert_bitcast_fusion = (bf16[16,8,128]{2,1,0:T(8,128)(2,1)S(1)}, bf16[16,8,128]{2,1,0:T(8,128)(2,1)S(1)}) fusion(f32[128,128]{1,0:T(8,128)} %get-tuple-element.5, f32[128,128]{1,0:T(8,128)} %get-tuple-element.4), kind=kLoop, calls=%fused_computation.16 | loop fusion | flops 32768 | bytes 196608 | tf_op jit(solution)/shard_map/convert.4
  59.1 1.5 %constant_dynamic-slice_fusion = f32[16,4,128]{2,1,0:T(4,128)} fusion(f32[16,8,128]{2,1,0:T(8,128)} %bitcast.56, s32[]{:T(128)S(6)} %select_n.6), kind=kLoop, calls=%fused_computation.35 | loop fusion | bytes 65540 | tf_op jit(solution)/shard_map/dynamic_slice | solution.py:374
  60.6 0.1 fusion.10
  60.6 0.1 fusion.7
  60.8 0.1 constant_dynamic-update-slice_fusion.7
  60.9 0.1 constant_dynamic-update-slice_fusion.6
  61.0 0.1 constant_dynamic-update-slice_fusion.4
  61.1 0.1 constant_dynamic-update-slice_fusion.3
  61.2 0.1 constant_dynamic-update-slice_fusion.1
  61.3 0.1 constant_dynamic-update-slice_fusion
  61.4 0.0 copy-done
  61.4 1.3 %multiply_convert_fusion = bf16[512,512]{1,0:T(8,128)(2,1)} fusion(bf16[144,512]{1,0:T(8,128)(2,1)S(1)} %copy-done, bf16[18,8,4,128]{3,2,1,0:T(4,128)(2,1)S(1)} %bitcast.58), kind=kOutput, calls=%fused_computation | convolution fusion | flops 76808192 | bytes 819200 | tf_op jit(solution)/shard_map/dot_general | solution.py:353
  (3 shorter events, 0.1 us)
Async XLA Ops:
  0.6 60.8 %copy-start = (bf16[144,512]{1,0:T(8,128)(2,1)S(1)}, bf16[144,512]{1,0:T(8,128)(2,1)}, u32[]{:S(2)}) copy-start(bf16[144,512]{1,0:T(8,128)(2,1)} %param.19) | copy-start | bytes 442372

commit v4 on v3

--- a/solution.py
+++ b/solution.py
@@ -42,8 +42,8 @@
 def fold_rows(modulation, w_patch, depth, w):
     patch = w_patch[...].astype(jnp.float32)
     patch = patch - jnp.mean(patch, axis=1, keepdims=True)
-    shift = jnp.broadcast_to(modulation[0:1], (16, patch.shape[1]))
-    rows = jnp.concatenate([patch * (1.0 + modulation[1:2]), shift], axis=0)
+    shift = jnp.broadcast_to(modulation[0], (16, patch.shape[1]))
+    rows = jnp.concatenate([patch * (1.0 + modulation[1]), shift], axis=0)
     total = rows.shape[1]
     rows = pltpu.roll(rows, lax.rem(total - w * depth, total), 1)[:, :depth]
     high = rows.astype(jnp.bfloat16)
@@ -52,11 +52,11 @@
 
 def step_kernel(
     groups, n,
-    offset_ref, sigma, latent, counts, mod, w_patch, w_final, w_qkv_hbm, w_out_hbm,
+    starts, step_index, latent, counts, mod, w_patch, w_final, w_qkv_hbm, w_out_hbm,
     clean, border,
     w_qkv, w_out, high, low, soft, edges, softs, edge_pair, parts, arrived, full, shifts,
     pat, rstd, att, turned_v, v, other, outgoing, incoming,
-    load_sem, send_a, recv_a, send_b, recv_b, send_x, recv_x, send_v, recv_v, send, recv,
+    load_sem, send_a, recv_a, send_c, send_b, recv_b, send_x, recv_x, send_v, recv_v, send, recv,
 ):
     g = lax.axis_index("groups")
     w = lax.axis_index("width")
@@ -87,6 +87,9 @@
     own = latent[...]
     soft[...] = own.astype(jnp.bfloat16)
     turned = own.T
+    index = jnp.full((1, columns), step_index[0], jnp.int32).astype(jnp.float32)
+    fraction = (index + 1.0) / STEPS
+    sigma = 3.0 * fraction / (1.0 + 2.0 * fraction)
     cover = counts[...].astype(jnp.float32)
     edges[...] = jnp.concatenate(
         [turned[:1], turned[columns - 1 :], cover, jnp.zeros((5, columns), jnp.float32)], axis=0
@@ -144,20 +147,39 @@
 
     full[me] = lax.fori_loop(1, n, add, parts[0].astype(jnp.float32)).astype(jnp.bfloat16)
 
-    def shared(step, peer, source):
+    deep = n // 2
+    sides = 2 * groups
+    side = g * 2 + lax.rem(w, 2)
+    level = w // 2
+
+    def owner_of(which_side, which_level):
+        return (which_side // 2) * n + which_level * 2 + lax.rem(which_side, 2)
+
+    def passed(source, peer, sent):
         return pltpu.make_async_remote_copy(
-            src_ref=full.at[source], dst_ref=full.at[source],
-            send_sem=send_b.at[step], recv_sem=recv_b.at[step],
+            src_ref=full.at[source], dst_ref=full.at[source], send_sem=sent, recv_sem=recv_b.at[source],
             device_id=at(peer // n, lax.rem(peer, n)), device_id_type=MESH,
         )
 
-    @pl.loop(1, owners)
-    def _(step):
-        shared(step, lax.rem(me + step, owners), me).start()
+    def along(step):
+        return passed(me, owner_of(side, lax.rem(level + step, deep)), send_c.at[step])
+
+    def aside(step, turn):
+        source = owner_of(side, lax.rem(level + step, deep))
+        peer = owner_of(lax.rem(side + turn, sides), level)
+        return passed(source, peer, send_b.at[step, turn])
+
+    @pl.loop(1, deep)
+    def _(step):
+        along(step).start()
+
+    @pl.loop(1, sides)
+    def _(turn):
+        aside(0, turn).start()
 
     for move in moves:
         move.wait()
-    offset = offset_ref[0]
+    offset = starts[0] - w * columns
     wide = jnp.concatenate([soft[...], softs[0], softs[1]], axis=1)
     wide = dot(row_map((area, area), 1, channels, height), wide).astype(jnp.bfloat16)
     spread = [dot(wide, column_map((3 * columns, columns), 0, b, offset)) for b in range(2)]
@@ -171,6 +193,16 @@
             axis=0,
         )
         pat[p * columns : (p + 1) * columns] = block.T.astype(jnp.bfloat16)
+
+    @pl.loop(1, deep)
+    def _(step):
+        source = owner_of(side, lax.rem(level + step, deep))
+        passed(source, source, send_c.at[step]).wait_recv()
+
+        @pl.loop(1, sides)
+        def _(turn):
+            aside(step, turn).start()
+
     tokens = pat.shape[0]
     step_rows = 2 * columns
     for start in range(0, tokens, step_rows):
@@ -188,10 +220,16 @@
     scale = math.log2(math.e) / math.sqrt(HEAD)
     ones = jnp.ones((tokens, HEAD), jnp.bfloat16)
 
-    @pl.loop(1, owners)
-    def _(step):
-        source = lax.rem(me - step + owners, owners)
-        shared(step, source, source).wait_recv()
+    def await_piece(source):
+        own_side = (source // n) * 2 + lax.rem(source, 2)
+
+        @pl.when(own_side != side)
+        def _():
+            passed(source, source, send_c.at[0]).wait_recv()
+
+    @pl.loop(pieces, owners)
+    def _(source):
+        await_piece(source)
 
     shifts[...] = full[pieces].astype(jnp.float32)
 
@@ -204,6 +242,8 @@
 
     @pl.loop(0, each)
     def _(j):
+        for i in range(3):
+            await_piece(i * each + j)
         queries = (head_norm(project(j)) * scale).astype(jnp.bfloat16)
         keys = head_norm(project(each + j)).astype(jnp.bfloat16)
         values = project(2 * each + j).astype(jnp.bfloat16)
@@ -224,7 +264,7 @@
     load_out.wait()
     for start in range(0, tokens, step_rows):
         rows = slice(start, start + step_rows)
-        residual = dot(pat[rows], w_patch[...]) + mod[2:3] * dot(att[rows], w_out[...])
+        residual = dot(pat[rows], w_patch[...]) + mod[2] * dot(att[rows], w_out[...])
         centered = residual - jnp.mean(residual, axis=1, keepdims=True)
         spread_of = jnp.mean(centered * centered, axis=1, keepdims=True)
         final_in = (centered * lax.rsqrt(spread_of + epsilon)).astype(jnp.bfloat16)
@@ -271,15 +311,21 @@
     def _(step):
         scatter(step).wait_send()
 
-    @pl.loop(1, owners)
-    def _(step):
-        shared(step, lax.rem(me + step, owners), me).wait_send()
+    @pl.loop(1, deep)
+    def _(step):
+        along(step).wait_send()
+
+    @pl.loop(0, deep)
+    def _(step):
+        @pl.loop(1, sides)
+        def _(turn):
+            aside(step, turn).wait_send()
 
     for move in moves:
         move.wait()
     got = [incoming[i].astype(jnp.float32) for i in range(4)]
     total = here + got[0] + jnp.where(at_end, 0.0, got[2])
-    clean[...] = own - sigma[0] * (total / cover)
+    clean[...] = own - sigma * (total / cover)
     around = jnp.where(at_end, got[1] + got[2], got[3] + ahead + got[1])
     row_end = lax.broadcasted_iota(jnp.int32, (1, columns), 1) == columns - 1
     right_edges, left_edges = edge_pair[0], edge_pair[1]
@@ -287,10 +333,10 @@
     beside = jnp.where(at_end, left_edges.T[:, 1:2], right_edges.T[:, 0:1])
     left = jnp.where(w > 0, 1.0, 0.0)
     right = jnp.where(w < n - 1, 1.0, 0.0)
-    border[...] = jnp.where(at_end, left, right) * (beside - sigma[0] * (around / covered))
-
-
-def run_step(groups, n, offset, sigma, own, counts, mod, w_patch, w_final, w_qkv, w_out):
+    border[...] = jnp.where(at_end, left, right) * (beside - sigma * (around / covered))
+
+
+def run_step(groups, n, starts, step_index, own, counts, mod, w_patch, w_final, w_qkv, w_out):
     total = w_qkv.shape[1]
     owners = groups * n
     size = LANES * -(-total // (LANES * owners))
@@ -331,13 +377,13 @@
             pltpu.VMEM((area, 3 * columns), half),
             pltpu.VMEM((4, *own.shape), half),
             pltpu.VMEM((4, *own.shape), half),
-            dma((2,)), dma((n,)), dma((n,)), dma((owners,)), dma((owners,)), dma((4,)), dma((4,)),
+            dma((2,)), dma((n,)), dma((n,)), dma((n // 2,)), dma((n // 2, 2 * groups)), dma((owners,)), dma((4,)), dma((4,)),
             dma, dma, dma((4,)), dma((4,)),
         ],
         compiler_params=pltpu.CompilerParams(
             collective_id=0, has_side_effects=True, vmem_limit_bytes=56 << 20
         ),
-    )(offset, sigma, own, counts, mod, w_patch, w_final, w_qkv, w_out)
+    )(starts, step_index, own, counts, mod, w_patch, w_final, w_qkv, w_out)
 
 
 def convolve(padded, w_dec):
@@ -359,15 +405,11 @@
 def shards(latent, starts, counts, step_index, cond_mod, w_patch, w_qkv, w_out, w_final, w_dec):
     groups, n = lax.axis_size("groups"), lax.axis_size("width")
     guide_at = lax.axis_index("guide")
-    place = lax.axis_index("width")
     channels, height, columns = latent.shape
     half_rows = height // 2
-    fraction = (step_index.astype(jnp.float32) + 1.0) / STEPS
-    sigma = 3.0 * fraction / (1.0 + 2.0 * fraction)
     own = latent.reshape(channels * height, columns)
-    offset = starts - place * columns
     clean, border = run_step(
-        groups, n, offset, sigma, own, counts[None], cond_mod[0], w_patch, w_final.T, w_qkv, w_out
+        groups, n, starts, step_index, own, counts[None], cond_mod.transpose(1, 0, 2), w_patch, w_final.T, w_qkv, w_out
     )
     rows = clean.reshape(latent.shape)
     sides = border.reshape(latent.shape)

time: 63 us -> 57.4 us (0.911)
  Pallas kernels: 54.8 us -> 50.6 us
  local copies, waits for them, and re-layouts: 3.57 us -> 2.2 us
    pallas_call x1, Pallas kernels: 54.8 us -> 50.6 us  [run_step(): pl.pallas_call(functools.partial(step_kernel, groups, n), name='guided_st...]
    unnamed x11 -> x10, local copies, waits for them, and re-layouts: 1.92 us -> 0.55 us
where the time goes in v4:
time: 57.4 us; the launch traced here: 57.1 us
  Pallas kernels  50.6 us (88%)
  local copies, waits for them, and re-layouts  2.2 us (4%)
  between operations  2.01 us (4%)
  matrix products  1.29 us (2%)
  other arithmetic  1.01 us (2%)
    pallas_call x1, Pallas kernels, run_step(): pl.pallas_call(functools.partial(step_kernel, groups, n), name='guided_st...  50.6 us
    dynamic_slice x1, local copies, waits for them, and re-layouts, shards(): lax.dynamic_slice_in_dim(rows, guide_at * half_rows, half_rows, 1)  1.47 us
    dot_general x1, matrix products, convolve(): lax.dot_general(stacked, w_dec, (((0,), (0,)), ((), ())), preferred_eleme...  1.29 us

profile of v4, /device:TPU:0, one launch (start us, length us, event | category | flops | bytes accessed | tf_op | source)
XLA Modules:
  0.0 57.1 jit_solution(8900833743679027834)
XLA Ops:
  0.6 0.0 copy-start
  2.0 50.6 %guided_step.1 = (f32[128,128]{1,0:T(8,128)}, f32[128,128]{1,0:T(8,128)}) custom-call(s32[1]{0:T(128)S(6)} %copy.25.starts, s32[1]{0:T(128)S(6)} %copy.26.step_index, f32[128,128]{1,0:T(8,128)} %bitcast.53, s32[1,128]{1,0:T(1,128)} %bitcast.56, f32[3,1,2432]{2,1,0:T(1,128)} %bitcast.54, bf16[64,2432]{1,0:T(8,128)(2,1)} %w_patch.1, ...), custom_call_target="tpu_custom_call" | custom-call | tf_op jit(solution)/shard_map/guided_step/pallas_call | solution.py:353
  52.6 0.9 %convert_bitcast_fusion = (bf16[16,8,128]{2,1,0:T(8,128)(2,1)S(1)}, bf16[16,8,128]{2,1,0:T(8,128)(2,1)S(1)}) fusion(f32[128,128]{1,0:T(8,128)} %get-tuple-element.5, f32[128,128]{1,0:T(8,128)} %get-tuple-element.4), kind=kLoop, calls=%fused_computation.15 | loop fusion | flops 32768 | bytes 196608 | tf_op jit(solution)/shard_map/convert.4
  53.5 1.5 %constant_dynamic-slice_fusion = f32[16,4,128]{2,1,0:T(4,128)} fusion(f32[16,8,128]{2,1,0:T(8,128)} %bitcast.52, s32[]{:T(128)S(6)} %select_n.6), kind=kLoop, calls=%fused_computation.34 | loop fusion | bytes 65540 | tf_op jit(solution)/shard_map/dynamic_slice | solution.py:416
  55.0 0.1 fusion.10
  55.1 0.1 fusion.7
  55.2 0.1 constant_dynamic-update-slice_fusion.7
  55.3 0.1 constant_dynamic-update-slice_fusion.6
  55.4 0.1 constant_dynamic-update-slice_fusion.4
  55.5 0.1 constant_dynamic-update-slice_fusion.3
  55.6 0.1 constant_dynamic-update-slice_fusion.1
  55.7 0.1 constant_dynamic-update-slice_fusion
  55.8 0.0 copy-done
  55.9 1.3 %multiply_convert_fusion = bf16[512,512]{1,0:T(8,128)(2,1)} fusion(bf16[144,512]{1,0:T(8,128)(2,1)S(1)} %copy-done, bf16[18,8,4,128]{3,2,1,0:T(4,128)(2,1)S(1)} %bitcast.55), kind=kOutput, calls=%fused_computation | convolution fusion | flops 76808192 | bytes 819200 | tf_op jit(solution)/shard_map/dot_general | solution.py:399
  (3 shorter events, 0.1 us)
Async XLA Ops:
  0.6 55.2 %copy-start = (bf16[144,512]{1,0:T(8,128)(2,1)S(1)}, bf16[144,512]{1,0:T(8,128)(2,1)}, u32[]{:S(2)}) copy-start(bf16[144,512]{1,0:T(8,128)(2,1)} %param.19) | copy-start | bytes 442372

commit v5 on v4

--- a/solution.py
+++ b/solution.py
@@ -52,10 +52,10 @@
 
 def step_kernel(
     groups, n,
-    starts, step_index, latent, counts, mod, w_patch, w_final, w_qkv_hbm, w_out_hbm,
-    clean, border,
+    starts, step_index, latent, counts, mod, w_patch, w_final, w_dec, w_qkv_hbm, w_out_hbm,
+    clean, feats,
     w_qkv, w_out, high, low, soft, edges, softs, edge_pair, parts, arrived, full, shifts,
-    pat, rstd, att, turned_v, v, other, outgoing, incoming,
+    pat, rstd, att, turned_v, v, other, outgoing, incoming, taps,
     load_sem, send_a, recv_a, send_c, send_b, recv_b, send_x, recv_x, send_v, recv_v, send, recv,
 ):
     g = lax.axis_index("groups")
@@ -325,7 +325,10 @@
         move.wait()
     got = [incoming[i].astype(jnp.float32) for i in range(4)]
     total = here + got[0] + jnp.where(at_end, 0.0, got[2])
-    clean[...] = own - sigma * (total / cover)
+    done = own - sigma * (total / cover)
+    half = height // 2
+    grid = done.reshape(channels, height, columns)
+    clean[...] = jnp.where(first, grid[:, :half], grid[:, half:])
     around = jnp.where(at_end, got[1] + got[2], got[3] + ahead + got[1])
     row_end = lax.broadcasted_iota(jnp.int32, (1, columns), 1) == columns - 1
     right_edges, left_edges = edge_pair[0], edge_pair[1]
@@ -333,10 +336,31 @@
     beside = jnp.where(at_end, left_edges.T[:, 1:2], right_edges.T[:, 0:1])
     left = jnp.where(w > 0, 1.0, 0.0)
     right = jnp.where(w < n - 1, 1.0, 0.0)
-    border[...] = jnp.where(at_end, left, right) * (beside - sigma * (around / covered))
-
-
-def run_step(groups, n, starts, step_index, own, counts, mod, w_patch, w_final, w_qkv, w_out):
+    border = jnp.where(at_end, left, right) * (beside - sigma * (around / covered))
+    moved = row_map((area, area), 1, channels, height)
+    center = dot(moved, done.astype(jnp.bfloat16))
+    border = dot(moved, border.astype(jnp.bfloat16))
+    at_start = lax.broadcasted_iota(jnp.int32, (area, columns), 1) == 0
+    before = jnp.where(at_start, pltpu.roll(border, 1, 1), pltpu.roll(center, 1, 1))
+    after = jnp.where(
+        at_end, pltpu.roll(border, columns - 1, 1), pltpu.roll(center, columns - 1, 1)
+    )
+    empty = jnp.zeros((channels, columns), jnp.bfloat16)
+    for b, tap in enumerate((before, center, after)):
+        taps[b, :channels] = empty
+        taps[b, channels : channels + area] = tap.astype(jnp.bfloat16)
+        taps[b, channels + area :] = empty
+    for i in range(half):
+        cuts = []
+        for a in range(3):
+            row = pl.multiple_of((e * half + i + a) * channels, channels)
+            cuts += [taps[b, pl.ds(row, channels)] for b in range(3)]
+        stacked = jnp.concatenate(cuts, axis=0).astype(jnp.float32).T.astype(jnp.bfloat16)
+        summed = dot(stacked, w_dec[...])
+        feats[i] = (summed / (1.0 + jnp.exp(-summed))).astype(jnp.bfloat16)
+
+
+def run_step(groups, n, starts, step_index, own, counts, mod, w_patch, w_final, w_dec, w_qkv, w_out):
     total = w_qkv.shape[1]
     owners = groups * n
     size = LANES * -(-total // (LANES * owners))
@@ -344,6 +368,8 @@
         size += LANES
     area, columns = own.shape
     features = w_patch.shape[0]
+    channels = features // 4
+    height = area // channels
     tokens = area * 2 * columns // features
     dma = pltpu.SemaphoreType.DMA
     vmem = pl.BlockSpec(memory_space=pltpu.VMEM)
@@ -353,8 +379,11 @@
     return pl.pallas_call(
         functools.partial(step_kernel, groups, n),
         name="guided_step",
-        out_shape=(jax.ShapeDtypeStruct(own.shape, own.dtype),) * 2,
-        in_specs=[smem] * 2 + [vmem] * 5 + [hbm] * 2,
+        out_shape=(
+            jax.ShapeDtypeStruct((channels, height // 2, columns), single),
+            jax.ShapeDtypeStruct((height // 2, columns, w_dec.shape[1]), half),
+        ),
+        in_specs=[smem] * 2 + [vmem] * 6 + [hbm] * 2,
         out_specs=(vmem, vmem),
         scratch_shapes=[
             pltpu.VMEM(w_qkv.shape, half),
@@ -377,48 +406,24 @@
             pltpu.VMEM((area, 3 * columns), half),
             pltpu.VMEM((4, *own.shape), half),
             pltpu.VMEM((4, *own.shape), half),
+            pltpu.VMEM((3, area + 2 * channels, columns), half),
             dma((2,)), dma((n,)), dma((n,)), dma((n // 2,)), dma((n // 2, 2 * groups)), dma((owners,)), dma((4,)), dma((4,)),
             dma, dma, dma((4,)), dma((4,)),
         ],
         compiler_params=pltpu.CompilerParams(
             collective_id=0, has_side_effects=True, vmem_limit_bytes=56 << 20
         ),
-    )(starts, step_index, own, counts, mod, w_patch, w_final, w_qkv, w_out)
-
-
-def convolve(padded, w_dec):
-    channels = padded.shape[0]
-    height = padded.shape[1] - 2
-    breadth = padded.shape[2] - 2
-    shifted = [
-        padded[:, row_at : row_at + height, col_at : col_at + breadth]
-        for row_at in range(3)
-        for col_at in range(3)
-    ]
-    stacked = jnp.stack(shifted).reshape(9 * channels, height * breadth)
-    summed = lax.dot_general(
-        stacked, w_dec, (((0,), (0,)), ((), ())), preferred_element_type=jnp.float32
-    )
-    return jax.nn.silu(summed).astype(jnp.bfloat16).reshape(height, breadth, w_dec.shape[1])
+    )(starts, step_index, own, counts, mod, w_patch, w_final, w_dec, w_qkv, w_out)
 
 
 def shards(latent, starts, counts, step_index, cond_mod, w_patch, w_qkv, w_out, w_final, w_dec):
     groups, n = lax.axis_size("groups"), lax.axis_size("width")
-    guide_at = lax.axis_index("guide")
     channels, height, columns = latent.shape
-    half_rows = height // 2
     own = latent.reshape(channels * height, columns)
-    clean, border = run_step(
-        groups, n, starts, step_index, own, counts[None], cond_mod.transpose(1, 0, 2), w_patch, w_final.T, w_qkv, w_out
+    return run_step(
+        groups, n, starts, step_index, own, counts[None], cond_mod.transpose(1, 0, 2),
+        w_patch, w_final.T, w_dec, w_qkv, w_out,
     )
-    rows = clean.reshape(latent.shape)
-    sides = border.reshape(latent.shape)
-    denoised = lax.dynamic_slice_in_dim(rows, guide_at * half_rows, half_rows, 1)
-    padded = jnp.concatenate([sides[:, :, -1:], rows, sides[:, :, :1]], axis=2).astype(jnp.bfloat16)
-    padded = jnp.pad(padded, ((0, 0), (1, 1), (0, 0)))
-    padded = lax.dynamic_slice_in_dim(padded, guide_at * half_rows, half_rows + 2, 1)
-    features = convolve(padded, w_dec)
-    return (denoised, features)
 
 
 def solution(mesh):

time: 57.4 us -> 57 us (level)
  matrix products: 1.29 us -> 0 us
  local copies, waits for them, and re-layouts: 2.2 us -> 3.24 us
  other arithmetic: 1.01 us -> 0 us
  Pallas kernels: 50.6 us -> 51.5 us
    unnamed x10 -> x2, local copies, waits for them, and re-layouts: 0.55 us -> 3.24 us
    dynamic_slice x1 -> x0, local copies, waits for them, and re-layouts: 1.47 us -> none  [shards(): lax.dynamic_slice_in_dim(rows, guide_at * half_rows, half_rows, 1)]
    dot_general x1 -> x0, matrix products: 1.29 us -> none  [convolve(): lax.dot_general(stacked, w_dec, (((0,), (0,)), ((), ())), preferred_eleme...]
    pallas_call x1, Pallas kernels: 50.6 us -> 51.5 us  [run_step(): pl.pallas_call(functools.partial(step_kernel, groups, n), name='guided_st...]
    another operation x1 -> x0, other arithmetic: 0.88 us -> none
where the time goes in v5:
time: 57 us; the launch traced here: 56.7 us
  Pallas kernels  51.5 us (90%)
  local copies, waits for them, and re-layouts  3.24 us (6%)
  between operations  1.93 us (3%)
    pallas_call x1, Pallas kernels, run_step(): pl.pallas_call(functools.partial(step_kernel, groups, n), name='guided_st...  51.5 us
    unnamed x2, local copies, waits for them, and re-layouts  3.24 us

profile of v5, /device:TPU:0, one launch (start us, length us, event | category | flops | bytes accessed | tf_op | source)
XLA Modules:
  0.0 56.7 jit_solution(13136990935961986108)
XLA Ops:
  1.9 51.5 %guided_step.1 = (f32[16,4,128]{2,1,0:T(4,128)}, bf16[4,128,512]{2,1,0:T(8,128)(2,1)}) custom-call(s32[1]{0:T(128)S(6)} %copy.14.starts, s32[1]{0:T(128)S(6)} %copy.15.step_index, f32[128,128]{1,0:T(8,128)} %bitcast.5, s32[1,128]{1,0:T(1,128)} %bitcast.7, f32[3,1,2432]{2,1,0:T(1,128)} %bitcast.6, bf16[64,2432]{1,0:T(8,128)(2,1)} %w_patch.1, ...), custom_call_target="tpu_custom_call" | custom-call | tf_op jit(solution)/shard_map/guided_step/pallas_call | solution.py:379
  53.5 1.4 %copy.16 = f32[16,4,128]{2,1,0:T(4,128)} copy(f32[16,4,128]{2,1,0:T(4,128)} %get-tuple-element.4) | data formatting | bytes 65536
  54.8 1.9 %copy.17 = bf16[4,128,512]{2,1,0:T(8,128)(2,1)} copy(bf16[4,128,512]{2,1,0:T(8,128)(2,1)} %get-tuple-element.5) | data formatting | bytes 1048576
